TPU v7x, 256 devices: a whole 4x4x8 slice. The times are simulated.
256 devices in a mesh: half: 2 (over core), prow: 16 (over z, x_hi), pcol: 8 (over x_lo, y).
Axes of the slice: x: 4 (x_hi: 2, x_lo: 2; x = x_hi * 2 + x_lo), y: 4, z: 8, core: 2. Of those that a mesh axis runs over, the one named last changes fastest.
Arguments:
- child_update: float32 [2, 8192, 8192], P('half', 'prow', 'pcol'), may hold values from -6 to 6, as said below
- child_panel: float32 [2, 8192, 1024], P('half', 'prow'), may hold values from -3 to 3
- root_front: float32 [12288, 12288], P('prow', ('half', 'pcol')), may hold values from -29 to 6144, as said below
- index_map: int32 [2, 64], replicated, may hold values from 0 to 95, as said below
Outputs:
- root_next: float32 [12288, 12288], P('prow', ('half', 'pcol'))
Inputs may be any that keep to these rules, and one draw needn't show every extreme that they name: `child_update`: each child's matrix is symmetric. `root_front`: Symmetric. `index_map`: for each child the entries are distinct, and child 0 names the blocks 0 to 1. Of the 8 blocks of one process row of both children (blocks p * 4 on), at most 1 share one root process row v // 6; of the 8 blocks of one child process column (blocks q * 8 on), at most 1 share one root column group v // 6; both bounds are reached.
All inputs are finite; a program needn't handle non-finite values.
Results may differ from a plain program's by a relative error of at most 0.00016.
Values sent between devices are 32-bit elements; how exact they have to be, the bound alone decides.
A program may use at most 128 MiB of HBM per device.

v0:
```python
import jax
import jax.numpy as jnp
from jax import lax
from jax.sharding import PartitionSpec as P

BLK = 128
RP = 256


def spread_2(value, axis, source):
    kept = jnp.where(lax.axis_index(axis) == source, value, 0).astype(value.dtype)
    return lax.psum(kept, axis)


def ranking(labels, count):
    onehot = (labels[..., None] == jnp.arange(count, dtype=jnp.int32)).astype(jnp.int32)
    return jnp.sum((jnp.cumsum(onehot, axis=-2) - 1) * onehot, axis=-1)


def solve_rows(factor, raw_rows, global_rows):
    solved = lax.linalg.triangular_solve(
        factor, raw_rows, left_side=False, lower=True, transpose_a=True
    )
    leading = jnp.concatenate(
        [factor, jnp.zeros((raw_rows.shape[0] - RP, RP), jnp.float32)], axis=0
    )
    return jnp.where(global_rows[:, None] < RP, leading, solved)


def shards(child_update, child_panel, root_front, index_map):
    highest = lax.Precision.HIGHEST
    rows_dev = child_update.shape[1]
    cols_dev = child_update.shape[2]
    col_count = lax.axis_size("pcol")
    row_count = lax.axis_size("prow")
    row_ratio = row_count // col_count
    group_count = 2 * col_count
    column_index = lax.axis_index("pcol")
    child_index = lax.axis_index("half")
    row_index = lax.axis_index("prow")
    group_index = lax.axis_index(("half", "pcol"))
    own_panel = child_panel[0]
    pieces = []
    for offset in range(row_ratio):
        remote = spread_2(own_panel, "prow", column_index * row_ratio + offset)
        product = lax.dot_general(
            own_panel,
            remote,
            (((1,), (1,)), ((), ())),
            precision=highest,
            preferred_element_type=jnp.float32,
        )
        pieces.append(child_update[0, :, offset * rows_dev : (offset + 1) * rows_dev] - product)
    schur_part = jnp.concatenate(pieces, axis=1)
    root_rows = root_front.shape[0]
    root_cols = root_front.shape[1]
    child_blocks = rows_dev // BLK
    col_blocks = cols_dev // BLK
    row_blocks = root_rows // BLK
    group_cols = root_cols // BLK
    cap_col = max(1, col_blocks // group_count)
    cap_row = max(1, 2 * child_blocks // row_count)
    by_column = index_map.reshape(2, col_count, col_blocks)
    by_row = index_map.reshape(2, row_count, child_blocks)
    col_groups = by_column // group_cols
    col_ranks = ranking(col_groups, group_count)
    row_owners = by_row // row_blocks
    arrives = col_groups == group_index
    col_slots = by_column - group_index * group_cols
    col_place = (
        arrives[:, :, :, None, None]
        & (col_ranks[:, :, :, None, None] == jnp.arange(cap_col, dtype=jnp.int32)[:, None])
        & (col_slots[:, :, :, None, None] == jnp.arange(group_cols, dtype=jnp.int32))
    ).astype(jnp.float32)
    col_place = jnp.sum(col_place, axis=2)
    row_local = by_row - row_index * row_blocks
    local_onehot = (row_local[..., None] == jnp.arange(row_blocks, dtype=jnp.int32)).astype(
        jnp.float32
    )
    own_groups = col_groups[child_index, column_index]
    own_col_ranks = col_ranks[child_index, column_index]
    col_select = (
        (own_groups[None, None, :] == jnp.arange(group_count, dtype=jnp.int32)[:, None, None])
        & (own_col_ranks[None, None, :] == jnp.arange(cap_col, dtype=jnp.int32)[None, :, None])
    ).astype(jnp.float32)
    child_ranks = ranking(row_owners, row_count)
    own_owner = row_owners[child_index, row_index]
    own_rank = child_ranks[child_index, row_index]
    row_select = (
        (own_owner[None, None, :] == jnp.arange(row_count, dtype=jnp.int32)[:, None, None])
        & (own_rank[None, None, :] == jnp.arange(cap_row, dtype=jnp.int32)[None, :, None])
    ).astype(jnp.float32)
    outgoing_rows = jnp.einsum(
        "tri,iyk->tryk",
        row_select,
        schur_part.reshape(child_blocks, BLK, cols_dev),
        precision=highest,
    )
    arrived = lax.all_to_all(outgoing_rows, "prow", split_axis=0, concat_axis=0, tiled=True)
    arrived_tiles = arrived.reshape(row_count, cap_row, BLK, col_blocks, BLK)
    outgoing = jnp.einsum("guj,pryjk->gupryk", col_select, arrived_tiles, precision=highest)
    incoming = lax.all_to_all(outgoing, ("half", "pcol"), split_axis=0, concat_axis=0, tiled=True)
    incoming = incoming.reshape(2, col_count, cap_col, row_count, cap_row, BLK, BLK)
    slot_item = (
        (row_owners[:, :, None, :] == row_index)
        & (child_ranks[:, :, None, :] == jnp.arange(cap_row, dtype=jnp.int32)[None, None, :, None])
    ).astype(jnp.float32)
    row_place = jnp.einsum("cpri,cpiw->cprw", slot_item, local_onehot, precision=highest)
    spread = jnp.einsum("cqus,cqupryz->cprysz", col_place, incoming, precision=highest)
    extended = jnp.einsum("cprw,cprysz->wysz", row_place, spread, precision=highest)
    assembled = root_front + extended.reshape(root_rows, root_cols)
    global_rows = row_index * root_rows + jnp.arange(root_rows, dtype=jnp.int32)
    global_cols = group_index * root_cols + jnp.arange(root_cols, dtype=jnp.int32)
    group_ratio = row_count // group_count
    raw_panel = assembled[:, :RP]
    pivot_block = spread_2(assembled[:RP, :RP], "prow", 0)
    factor = jnp.linalg.cholesky(pivot_block)
    own_rows = solve_rows(factor, raw_panel, global_rows)
    row_panel = spread_2(own_rows, ("half", "pcol"), 0)
    offset = 0
    across = spread_2(row_panel, "prow", group_index * group_ratio + offset)
    update = lax.dot_general(
        row_panel,
        across,
        (((1,), (1,)), ((), ())),
        precision=highest,
        preferred_element_type=jnp.float32,
    )
    trailing_mask = (global_rows[:, None] >= RP) & (global_cols[None, :] >= RP)
    trailing = assembled - jnp.where(trailing_mask, update, 0.0)
    first_group = group_index == 0
    panel_cols = jnp.where(first_group, row_panel, trailing[:, :RP])
    return jnp.concatenate([panel_cols, trailing[:, RP:]], axis=1)


def solution(mesh):
    return jax.shard_map(
        shards,
        mesh=mesh,
        in_specs=(
            P("half", "prow", "pcol"),
            P("half", "prow", None),
            P("prow", ("half", "pcol")),
            P(),
        ),
        out_specs=P("prow", ("half", "pcol")),
        check_vma=False,
    )
```

profile of v0, /device:TPU:4, one launch (start us, length us, event | category | flops | bytes accessed | tf_op | source)
XLA Modules:
  0.0 1266.2 jit_solution(17898139743299591110)
XLA Ops:
  6.5 4.3 bitcast_select_fusion.1
  10.9 1.6 copy-done.4
  12.4 1.2 fusion.59
  13.6 1.3 copy.121
  15.0 1.6 copy.122
  16.9 0.1 copy.88
  17.0 0.2 dynamic-slice_reduce_fusion
  17.2 0.3 fusion.60
  17.5 0.2 fusion.53
  17.7 201.6 %all-reduce.14.cloned.1.call-done = (f32[512,1024]{1,0:T(8,128)}, f32[512,1024]{1,0:T(8,128)}) async-done(((f32[512,1024]{1,0:T(8,128)}, f32[512,1024]{1,0:T(8,128)}), (f32[512,1024]{1,0:T(8,128)}, f32[512,1024]{1,0:T(8,128)})) %all-reduce.14.cloned.1.call-update) | async-done | bytes 4194320 | tf_op jit(solution)/shard_map/psum | solution.py:12
  219.2 5.6 fusion.18
  224.8 3.6 fusion.24
  228.4 0.2 pad_maximum_fusion.1
  228.6 2.0 reshape.343
  230.6 3.0 copy.92
  233.6 4.1 convolution_bitcast_fusion.1
  237.7 8.1 copy.93
  245.7 10.1 all-to-all-start
  256.0 0.1 fusion.38
  256.2 0.4 select_reduce_fusion.3
  256.6 184.3 %all-to-all-done = f32[16,1,128,1024]{3,2,1,0:T(8,128)} async-done(((f32[16,1,128,1024]{3,2,1,0:T(8,128)}), f32[16,1,128,1024]{3,2,1,0:T(8,128)}, u32[]{:S(2)}, u32[]{:S(2)}) %all-to-all-start) | async-done | bytes 8388640 | tf_op jit(solution)/shard_map/all_to_all | solution.py:99
  440.9 5.5 copy.125
  446.4 8.2 convolution_bitcast_fusion
  454.6 10.7 copy.94
  465.3 5.5 all-to-all-start.1
  470.9 0.1 copy.123
  471.1 2.0 copy.98
  473.1 0.1 convert_reduce_fusion
  473.2 0.1 select_reduce_fusion
  473.3 198.9 %all-to-all-done.1 = f32[16,1,16,1,128,128]{5,4,2,3,1,0:T(8,128)} async-done(((f32[16,1,16,1,128,128]{5,4,2,3,1,0:T(8,128)}), f32[16,1,16,1,128,128]{5,4,2,3,1,0:T(8,128)}, u32[]{:S(2)}, u32[]{:S(2)}) %all-to-all-start.1) | async-done | bytes 16777248 | tf_op jit(solution)/shard_map/all_to_all | solution.py:102
  672.2 32.3 %fusion.5 = f32[2,16,128,6,128]{4,3,2,1,0:T(8,128)} fusion(f32[2,8,16,128,128]{4,3,2,1,0:T(8,128)} %bitcast.15, f32[2,8,6]{1,2,0:T(8,128)S(1)} %convert_reduce_fusion), kind=kOutput, calls=%fused_computation.8 | convolution fusion | flops 301989888 | bytes 29360512 | tf_op jit(solution)/shard_map/cqus,cqupryz->cprysz/dot_general | solution.py:109
  704.5 17.1 %fusion.12 = f32[6,128,6,128]{3,0,2,1:T(8,128)S(1)} fusion(f32[2,16,128,6,128]{4,3,2,1,0:T(8,128)} %fusion.5, f32[2,16,6]{2,1,0:T(8,128)S(1)} %select_reduce_fusion), kind=kOutput, calls=%fused_computation.20 | convolution fusion | flops 226492416 | bytes 14942976 | tf_op jit(solution)/shard_map/cprw,cprysz->wysz/dot_general | solution.py:110
  721.6 2.4 copy.118
  724.0 3.3 bitcast_add_fusion
  727.3 0.7 slice_select_fusion.1
  728.1 160.3 %all-reduce.8.cloned.1.call-done = f32[256,256]{0,1:T(8,128)} async-done(((f32[256,256]{0,1:T(8,128)}), f32[256,256]{0,1:T(8,128)}) %all-reduce.8.cloned.1.call-update) | async-done | bytes 262160 | tf_op jit(solution)/shard_map/psum | solution.py:12
  888.4 1.1 copy.100
  889.5 1.0 fusion.31
  890.5 11.7 cholesky.49
  902.3 9.8 custom-call.14
  912.1 0.2 fusion.35
  912.3 0.3 convolution_subtract_fusion.1
  912.6 11.7 cholesky.103
  924.4 0.1 copy.102
  924.5 0.1 copy.101
  924.6 0.7 compare_reduce_fusion
  926.9 4.5 while.1
  927.0 0.6 fusion.71
  927.6 1.4 dynamic-slice.7
  929.2 0.6 fusion.71
  929.8 1.4 dynamic-slice.7
  931.4 19.7 %custom-call.15 = f32[2,128,128]{1,2,0:T(8,128)S(1)} custom-call(f32[2,128,128]{2,1,0:T(8,128)S(1)} %get-tuple-element.12), custom_call_target="InvertDiagBlocksLowerTriangular" | custom-call | tf_op jit(solution)/shard_map/triangular_solve | solution.py:21
  951.1 0.5 fusion.29
  951.6 0.5 convolution_subtract_fusion
  952.1 0.5 fusion.33
  952.6 1.0 fusion.28
  953.7 134.8 %all-reduce.10.cloned.1.call-done = f32[768,256]{0,1:T(8,128)} async-done(((f32[768,256]{0,1:T(8,128)}), f32[768,256]{0,1:T(8,128)}) %all-reduce.10.cloned.1.call-update) | async-done | bytes 786448 | tf_op jit(solution)/shard_map/psum | solution.py:12
  1088.5 0.9 broadcast_select_fusion
  1089.5 164.0 %all-reduce.12.cloned.1.call-done = f32[768,256]{0,1:T(8,128)} async-done(((f32[768,256]{0,1:T(8,128)}), f32[768,256]{0,1:T(8,128)}) %all-reduce.12.cloned.1.call-update) | async-done | bytes 786448 | tf_op jit(solution)/shard_map/psum | solution.py:12
  1253.6 3.6 select_subtract_fusion
  1257.2 0.1 slice.78
  1257.3 0.1 slice_select_fusion
  1257.4 0.2 pad_maximum_fusion
  1257.5 2.0 copy.106
  (55 shorter events, 1.5 us)
Async XLA Ops:
  6.5 212.7 %all-reduce.14.cloned.1.call-start = ((), (), s32[]{:S(2)}) async-start(), calls=%async_computation.5 | async-start | bytes 8388608 | tf_op jit(solution)/shard_map/psum | solution.py:12
  10.9 1.6 copy-start.4
  13.6 2.9 copy-start.5
  13.6 205.6 %copy-start = (f32[1,512,1024]{2,1,0:T(8,128)S(1)}, f32[1,512,1024]{2,1,0:T(8,128)}, u32[]{:S(2)}) copy-start(f32[1,512,1024]{2,1,0:T(8,128)} %param.5) | copy-start | bytes 6291460
  219.2 5.6 copy-start.3
  245.7 195.2 %all-to-all-start = ((f32[16,1,128,1024]{3,2,1,0:T(8,128)}), f32[16,1,128,1024]{3,2,1,0:T(8,128)}, u32[]{:S(2)}, u32[]{:S(2)}) async-start(f32[16,1,128,1024]{3,2,1,0:T(8,128)} %copy.93), calls=%async_computation | async-start | bytes 16777216 | tf_op jit(solution)/shard_map/all_to_all | solution.py:99
  465.3 5.8 copy-start.2
  465.3 206.9 %all-to-all-start.1 = ((f32[16,1,16,1,128,128]{5,4,2,3,1,0:T(8,128)}), f32[16,1,16,1,128,128]{5,4,2,3,1,0:T(8,128)}, u32[]{:S(2)}, u32[]{:S(2)}) async-start(f32[16,1,16,1,128,128]{5,4,2,3,1,0:T(8,128)} %copy.94), calls=%async_computation.1 | async-start | bytes 33554432 | tf_op jit(solution)/shard_map/all_to_all | solution.py:102
  470.8 417.6 %all-reduce.8.cloned.1.call-start = ((), (), s32[]{:S(2)}) async-start(), calls=%async_computation.2 | async-start | bytes 524288 | tf_op jit(solution)/shard_map/psum | solution.py:12
  728.0 360.5 %all-reduce.10.cloned.1.call-start = ((), (), s32[]{:S(2)}) async-start(), calls=%async_computation.3 | async-start | bytes 1572864 | tf_op jit(solution)/shard_map/psum | solution.py:12
  953.6 299.9 %all-reduce.12.cloned.1.call-start = ((), (), s32[]{:S(2)}) async-start(), calls=%async_computation.4 | async-start | bytes 1572864 | tf_op jit(solution)/shard_map/psum | solution.py:12
  1088.5 165.0 %copy-start.1 = (f32[768,256]{0,1:T(8,128)S(1)}, f32[768,256]{0,1:T(8,128)}, u32[]{:S(2)}) copy-start(f32[768,256]{0,1:T(8,128)} %all-reduce.10.cloned.1.call-done) | copy-start | bytes 2359300
Sparse Core Ops, SparseCore 0:
  11.0 208.1 all-reduce.13
  728.2 160.2 all-reduce.7
  953.7 134.7 all-reduce.9
  1091.0 162.5 all-reduce.11
where the time goes:
time: 1270 us
  waiting for transfers between devices  1040 us (82%)
  matrix products  76.4 us (6%)
  other arithmetic  66.8 us (5%)
  local copies, waits for them, and re-layouts  47.9 us (4%)
  starting transfers between devices  15.7 us (1%)
  between operations  15.1 us (1%)
    psum x4, waiting for transfers between devices, spread_2(): return lax.psum(kept, axis)  661 us
    all_to_all x1, waiting for transfers between devices, shards(): lax.all_to_all(outgoing, ('half', 'pcol'), split_axis=0, concat_axis=0, t...  199 us
    all_to_all x1, waiting for transfers between devices, shards(): lax.all_to_all(outgoing_rows, 'prow', split_axis=0, concat_axis=0, tiled=...  184 us
    another operation x6, other arithmetic, shards(): factor = jnp.linalg.cholesky(pivot_block)  34 us
    dot_general x1, matrix products, shards(): jnp.einsum('cqus,cqupryz->cprysz', col_place, incoming, precision=highest)  32.3 us
  transfers between devices with their start and end apart: 6, of which 6 were waited for; matrix products, arithmetic and copies ran while one was open for 1% of the time, Pallas kernels for 0%

commit v1 on v0

v1 whole, which is shorter than its diff:
```python
import functools

import jax
import jax.numpy as jnp
from jax import lax
from jax.experimental import pallas as pl
from jax.experimental.pallas import tpu as pltpu
from jax.sharding import PartitionSpec as P

BLK = 128
RP = 256
HALF = BLK // 2
NZ = 8
CHUNKS = 32
MESH = pl.DeviceIdType.MESH
ANY = pl.BlockSpec(memory_space=pl.ANY)


def position():
    return lax.axis_index("half"), lax.axis_index("prow"), lax.axis_index("pcol")


def greet(devices):
    barrier = pltpu.get_barrier_semaphore()
    for device in devices:
        pl.semaphore_signal(barrier, inc=1, device_id=device, device_id_type=MESH)
    pl.semaphore_wait(barrier, len(devices))


def spread_kernel(panel, out, local_sem, up_send, up_recv, down_send, down_recv, side_send):
    child, prow, pcol = position()
    z, x = prow // 2, prow % 2
    other_x = 1 - x
    up = (child, ((z + 1) % NZ) * 2 + x, pcol)
    down = (child, ((z + NZ - 1) % NZ) * 2 + x, pcol)
    side = (child, z * 2 + other_x, (pcol + 4) % 8)
    greet((up, down, side))
    rows = panel.shape[0] // CHUNKS
    above = (z + NZ - pcol) % NZ
    below = (pcol + NZ - z) % NZ
    from_side = z == (pcol + 4) % 8

    def piece(index):
        return pl.ds(pl.multiple_of(index * rows, rows), rows)

    def up_copy(index, source):
        return pltpu.make_async_remote_copy(
            source, out.at[x, piece(index)], up_send.at[index], up_recv.at[index],
            device_id=up, device_id_type=MESH)

    def down_copy(index):
        there = out.at[other_x, piece(index)]
        return pltpu.make_async_remote_copy(
            there, there, down_send.at[index], down_recv.at[index],
            device_id=down, device_id_type=MESH)

    def side_copy(index):
        return pltpu.make_async_remote_copy(
            panel.at[piece(index)], out.at[x, piece(index)], side_send.at[index],
            down_recv.at[index], device_id=side, device_id_type=MESH)

    own = pltpu.make_async_copy(panel, out.at[x], local_sem)

    @pl.when(from_side)
    def _():
        @pl.loop(0, CHUNKS)
        def _(index):
            side_copy(index).start()

    @pl.when(above == 0)
    def _():
        @pl.loop(0, CHUNKS)
        def _(index):
            up_copy(index, panel.at[piece(index)]).start()

        own.start()

    up_lag = (3 * above) // 2
    down_lag = (3 * below) // 2 + 1

    @pl.loop(0, CHUNKS + 12)
    def _(step):
        up_index = step - up_lag
        down_index = step - down_lag

        @pl.when((above > 0) & (up_index >= 0) & (up_index < CHUNKS))
        def _():
            copy = up_copy(up_index, out.at[x, piece(up_index)])
            copy.wait_recv()

            @pl.when(above < NZ - 1)
            def _():
                copy.start()

        @pl.when((down_index >= 0) & (down_index < CHUNKS))
        def _():
            copy = down_copy(down_index)
            copy.wait_recv()

            @pl.when(below < NZ - 1)
            def _():
                copy.start()

    @pl.when(above < NZ - 1)
    def _():
        @pl.loop(0, CHUNKS)
        def _(index):
            up_copy(index, panel.at[piece(index)]).wait_send()

    @pl.when(below < NZ - 1)
    def _():
        @pl.loop(0, CHUNKS)
        def _(index):
            down_copy(index).wait_send()

    @pl.when(from_side)
    def _():
        @pl.loop(0, CHUNKS)
        def _(index):
            side_copy(index).wait_send()

    @pl.when(above == 0)
    def _():
        own.wait()


def spread(panel):
    rows, cols = panel.shape
    sems = pltpu.SemaphoreType.DMA((CHUNKS,))
    return pl.pallas_call(
        spread_kernel,
        out_shape=jax.ShapeDtypeStruct((2, rows, cols), jnp.float32),
        in_specs=[ANY],
        out_specs=ANY,
        scratch_shapes=[pltpu.SemaphoreType.DMA] + [sems] * 5,
        compiler_params=pltpu.CompilerParams(collective_id=0, has_side_effects=True),
    )(panel)


def split(value):
    high = value.astype(jnp.bfloat16)
    return high, (value - high.astype(jnp.float32)).astype(jnp.bfloat16)


def dot3(left, right, dims):
    dot = functools.partial(
        lax.dot_general, dimension_numbers=(dims, ((), ())), preferred_element_type=jnp.float32)
    return dot(left[0], right[0]) + (dot(left[0], right[1]) + dot(left[1], right[0]))


def schur_kernel(panel, columns, update, out, high, low):
    @pl.when(pl.program_id(0) == 0)
    def _():
        high[...], low[...] = split(panel[...])

    product = dot3((high[...], low[...]), split(columns[...]), ((1,), (1,)))
    value = update[...] - product
    for block in range(out.shape[1]):
        for half in range(2):
            start = block * BLK + half * HALF
            out[half, block] = value[start : start + HALF]


def schur(panel, columns, update):
    rows, depth = panel.shape
    tile = 256
    width = update.shape[1]
    blocks = rows // BLK
    return pl.pallas_call(
        schur_kernel,
        out_shape=jax.ShapeDtypeStruct((2, blocks, HALF, width), jnp.float32),
        grid=(width // tile,),
        in_specs=[
            pl.BlockSpec((rows, depth), lambda n: (0, 0)),
            pl.BlockSpec((tile, depth), lambda n: (n, 0)),
            pl.BlockSpec((rows, tile), lambda n: (0, n)),
        ],
        out_specs=pl.BlockSpec((2, blocks, HALF, tile), lambda n: (0, 0, 0, n)),
        scratch_shapes=[pltpu.VMEM((rows, depth), jnp.bfloat16)] * 2,
    )(panel, columns, update)


def pick_kernel(index, source, out):
    out[...] = source[...]


def pick(index, source, count):
    block = (1,) + source.shape[1:]
    return pl.pallas_call(
        pick_kernel,
        out_shape=jax.ShapeDtypeStruct((count,) + source.shape[1:], jnp.float32),
        grid_spec=pltpu.PrefetchScalarGridSpec(
            num_scalar_prefetch=1,
            grid=(count,),
            in_specs=[pl.BlockSpec(block, lambda n, index: (index[n], 0, 0))],
            out_specs=pl.BlockSpec(block, lambda n, index: (n, 0, 0)),
        ),
    )(index, source)


def deal_kernel(rows, cols, arrived, out):
    child = pl.program_id(0)
    for group in range(out.shape[0]):
        start = pl.multiple_of(cols[child, group] * BLK, BLK)
        out[group, 0, 0] = arrived[0, :, pl.ds(start, BLK)]


def deal(rows, cols, arrived, groups, slots):
    width = arrived.shape[2]
    return pl.pallas_call(
        deal_kernel,
        out_shape=jax.ShapeDtypeStruct((groups, 2, slots, HALF, BLK), jnp.float32),
        grid_spec=pltpu.PrefetchScalarGridSpec(
            num_scalar_prefetch=2,
            grid=(2, slots),
            in_specs=[
                pl.BlockSpec((1, HALF, width), lambda c, i, rows, cols: (rows[c, i], 0, 0))],
            out_specs=pl.BlockSpec(
                (groups, 1, 1, HALF, BLK), lambda c, i, rows, cols: (0, c, i, 0, 0)),
        ),
    )(rows, cols, arrived)


def extend_kernel(source, row_there, col_there, root, *refs):
    parts, out = refs[:-1], refs[-1]
    column = pl.program_id(0)
    for slot in range(out.shape[0] // BLK):
        for half in range(2):
            rows = pl.ds(slot * BLK + half * HALF, HALF)
            value = root[rows, :]
            for child in range(2):
                there = row_there[child, slot] * col_there[child, column] > 0
                part = parts[child * 2 + half][0, 0, slot]
                value = value + jnp.where(there, part, 0.0)
            out[rows, :] = value


def extend(source, row_there, col_there, root, incoming):
    rows, cols = root.shape
    slots = cols // BLK
    groups = incoming.shape[0] // 2

    def part(child, half):
        return pl.BlockSpec(
            (1, 1, rows // BLK, HALF, BLK),
            lambda j, source, *_: (half * groups + source[child, j], child, 0, 0, 0))

    column = pl.BlockSpec((rows, BLK), lambda j, *_: (0, j))
    return pl.pallas_call(
        extend_kernel,
        out_shape=jax.ShapeDtypeStruct(root.shape, jnp.float32),
        grid_spec=pltpu.PrefetchScalarGridSpec(
            num_scalar_prefetch=3,
            grid=(slots,),
            in_specs=[column] + [part(c, h) for c in range(2) for h in range(2)],
            out_specs=column,
        ),
    )(source, row_there, col_there, root, *[incoming] * 4)


def share_kernel(row_raw, col_raw, row_out, col_out, pivot_out, local_sem, *sems):
    (row_in, row_cast, row_recv, row_send, col_in, col_cast, col_recv, col_send,
     pivot_in, pivot_cast, pivot_mid, pivot_down, pivot_recv, pivot_send) = sems
    half, prow, pcol = position()
    count = 16
    group = half * 8 + pcol

    def in_row(k):
        return (k // 8, prow, k % 8)

    def in_col(k):
        return (half, k, pcol)

    greet([in_row((group + k) % count) for k in range(1, count)]
          + [in_col((prow + k) % count) for k in range(1, count)])
    row_piece, col_piece, pivot_piece = row_out.shape[1], col_out.shape[1], pivot_out.shape[1]
    pivot_owner = (group == 0) & (prow == 0)

    def cut(ref, k, size):
        return ref.at[pl.ds(pl.multiple_of(k * size, size), size)]

    def remote(source, target, send, recv, device):
        return pltpu.make_async_remote_copy(
            source, target, send, recv, device_id=device, device_id_type=MESH)

    def others(me, body):
        @pl.loop(1, count)
        def _(step):
            body((me + step) % count)

    def pivot_first(k):
        return remote(cut(row_raw, k, pivot_piece), pivot_out.at[k], pivot_cast.at[k],
                      pivot_in, in_row(k))

    def pivot_second(k):
        return remote(pivot_out.at[group], pivot_out.at[group], pivot_down.at[k],
                      pivot_mid, in_col(k))

    def pivot_third(k):
        return remote(pivot_out.at[group], pivot_out.at[group], pivot_send.at[k],
                      pivot_recv.at[group], in_row(k))

    def row_first(k):
        return remote(cut(row_raw, k, row_piece), row_out.at[k], row_cast.at[k], row_in, in_row(k))

    def row_second(k):
        return remote(row_out.at[group], row_out.at[group], row_send.at[k], row_recv.at[group],
                      in_row(k))

    def col_first(k):
        return remote(cut(col_raw, k, col_piece), col_out.at[k], col_cast.at[k], col_in, in_col(k))

    def col_second(k):
        return remote(col_out.at[prow], col_out.at[prow], col_send.at[k], col_recv.at[prow],
                      in_col(k))

    @pl.when(pivot_owner)
    def _():
        others(group, lambda k: pivot_first(k).start())

    @pl.when(group == 0)
    def _():
        others(group, lambda k: row_first(k).start())

    @pl.when(prow == 0)
    def _():
        others(prow, lambda k: col_first(k).start())

    def keep(source, target, size):
        @pl.loop(0, count)
        def _(k):
            pltpu.make_async_copy(cut(source, k, size), target.at[k], local_sem).start()
        @pl.loop(0, count)
        def _(k):
            pltpu.make_async_copy(cut(source, k, size), target.at[k], local_sem).wait()

    @pl.when(pivot_owner)
    def _():
        keep(row_raw, pivot_out, pivot_piece)

    @pl.when(prow == 0)
    def _():
        @pl.when(group > 0)
        def _():
            pivot_first(group).wait_recv()

        others(prow, lambda k: pivot_second(k).start())

    @pl.when(group == 0)
    def _():
        keep(row_raw, row_out, row_piece)

    @pl.when(prow == 0)
    def _():
        keep(col_raw, col_out, col_piece)

    @pl.when(group > 0)
    def _():
        row_first(group).wait_recv()

    def skip_first(k, body):
        @pl.when(k > 0)
        def _():
            body()

    others(group, lambda k: skip_first(k, lambda: row_second(k).start()))

    @pl.when(prow > 0)
    def _():
        pivot_second(prow).wait_recv()

    def skip_owner(k, body):
        @pl.when((prow > 0) | (k > 0))
        def _():
            body()

    others(group, lambda k: skip_owner(k, lambda: pivot_third(k).start()))

    @pl.when(prow > 0)
    def _():
        col_first(prow).wait_recv()

    others(prow, lambda k: skip_first(k, lambda: col_second(k).start()))

    def arrive(target, recv, k):
        remote(target.at[k], target.at[k], local_sem, recv.at[k], in_row(k)).wait_recv()

    @pl.when(jnp.logical_not(pivot_owner))
    def _():
        others(group, lambda k: arrive(pivot_out, pivot_recv, k))

    @pl.when(group > 0)
    def _():
        others(group, lambda k: arrive(row_out, row_recv, k))

    @pl.when(prow > 0)
    def _():
        others(prow, lambda k: arrive(col_out, col_recv, k))

    @pl.when(pivot_owner)
    def _():
        others(group, lambda k: pivot_first(k).wait_send())

    @pl.when(group == 0)
    def _():
        others(group, lambda k: row_first(k).wait_send())

    @pl.when(prow == 0)
    def _():
        others(prow, lambda k: col_first(k).wait_send())
        others(prow, lambda k: pivot_second(k).wait_send())

    others(group, lambda k: skip_first(k, lambda: row_second(k).wait_send()))
    others(group, lambda k: skip_owner(k, lambda: pivot_third(k).wait_send()))
    others(prow, lambda k: skip_first(k, lambda: col_second(k).wait_send()))


def share(row_raw, col_raw):
    count = 16
    one, many = pltpu.SemaphoreType.DMA, pltpu.SemaphoreType.DMA((count,))
    rows, cols = row_raw.shape[0], col_raw.shape[1]
    row_out, col_out, pivot = pl.pallas_call(
        share_kernel,
        out_shape=(
            jax.ShapeDtypeStruct((count, rows // count, RP), jnp.float32),
            jax.ShapeDtypeStruct((count, RP // count, cols), jnp.float32),
            jax.ShapeDtypeStruct((count, RP // count, RP), jnp.float32),
        ),
        in_specs=[ANY, ANY],
        out_specs=(ANY, ANY, ANY),
        scratch_shapes=[one, one, many, many, many, one, many, many, many,
                        one, many, one, many, many, many],
        compiler_params=pltpu.CompilerParams(collective_id=1, has_side_effects=True),
    )(row_raw, col_raw)
    return row_out.reshape(rows, RP), col_out.reshape(RP, cols), pivot.reshape(RP, RP)


def find(labels, wanted, values):
    hit = labels[..., None, :] == wanted[:, None]
    return jnp.sum(jnp.where(hit, values, 0), axis=-1).astype(jnp.int32), jnp.any(hit, axis=-1)


def shards(child_update, child_panel, root_front, index_map):
    rows_dev, cols_dev = child_update.shape[1:]
    root_rows, root_cols = root_front.shape
    row_count, col_count, groups = 16, 8, 16
    row_index = lax.axis_index("prow")
    col_index = lax.axis_index("pcol")
    group_index = lax.axis_index(("half", "pcol"))
    row_slots, col_slots = root_rows // BLK, root_cols // BLK
    child_blocks, col_blocks = rows_dev // BLK, cols_dev // BLK
    blocks = jnp.arange(index_map.shape[1], dtype=jnp.int32)
    everyone = jnp.arange(row_count, dtype=jnp.int32)

    own_rows = lax.dynamic_slice_in_dim(index_map, row_index * child_blocks, child_blocks, 1)
    leaves, _ = find(own_rows.reshape(-1) // row_slots, everyone,
                     jnp.arange(2 * child_blocks, dtype=jnp.int32))
    row_source, row_there = find(
        index_map, row_index * row_slots + jnp.arange(row_slots, dtype=jnp.int32),
        blocks // child_blocks)
    own_cols = lax.dynamic_slice_in_dim(index_map, col_index * col_blocks, col_blocks, 1)
    col_leaves, _ = find(own_cols // col_slots, everyone, jnp.arange(col_blocks, dtype=jnp.int32))
    col_source, col_there = find(
        index_map, group_index * col_slots + jnp.arange(col_slots, dtype=jnp.int32),
        blocks // col_blocks)

    own_panel = child_panel[0]
    columns = spread(own_panel).reshape(cols_dev, -1)
    part = schur(own_panel, columns, child_update[0])
    both = lax.all_to_all(part, "half", split_axis=0, concat_axis=0, tiled=True)
    outgoing = pick(leaves, both.reshape(2 * child_blocks, HALF, cols_dev), row_count)
    arrived = lax.all_to_all(outgoing, "prow", split_axis=0, concat_axis=0, tiled=True)
    dealt = deal(row_source, col_leaves, arrived, groups, row_slots)
    incoming = lax.all_to_all(dealt, ("half", "pcol"), split_axis=0, concat_axis=0, tiled=True)
    assembled = extend(col_source, row_there.astype(jnp.int32), col_there.astype(jnp.int32),
                       root_front, incoming)

    high = lax.Precision.HIGH
    row_raw, col_raw, pivot = share(assembled[:, :RP], assembled[:RP, :])
    factor = jnp.linalg.cholesky(pivot)
    inverse = lax.linalg.triangular_solve(
        factor, jnp.eye(RP, dtype=jnp.float32), left_side=True, lower=True)
    global_rows = row_index * root_rows + jnp.arange(root_rows, dtype=jnp.int32)
    global_cols = group_index * root_cols + jnp.arange(root_cols, dtype=jnp.int32)
    left = lax.dot_general(row_raw, inverse, (((1,), (1,)), ((), ())), precision=high)
    right = lax.dot_general(inverse, col_raw, (((1,), (0,)), ((), ())), precision=high)
    update = lax.dot_general(left, right, (((1,), (0,)), ((), ())), precision=high)
    trailing_mask = (global_rows[:, None] >= RP) & (global_cols[None, :] >= RP)
    trailing = assembled - jnp.where(trailing_mask, update, 0.0)
    leading = jnp.pad(factor, ((0, root_rows - RP), (0, 0)))
    panel = jnp.where(global_rows[:, None] < RP, leading, left)
    panel_cols = jnp.where(group_index == 0, panel, trailing[:, :RP])
    return jnp.concatenate([panel_cols, trailing[:, RP:]], axis=1)


def solution(mesh):
    return jax.shard_map(
        shards,
        mesh=mesh,
        in_specs=(
            P("half", "prow", "pcol"),
            P("half", "prow", None),
            P("prow", ("half", "pcol")),
            P(),
        ),
        out_specs=P("prow", ("half", "pcol")),
        check_vma=False,
    )
```

time: 1270 us -> 501 us (0.39)
  waiting for transfers between devices: 1040 us -> 169 us
  Pallas kernels: 0 us -> 186 us
  matrix products: 76.4 us -> 8.42 us
  starting transfers between devices: 15.7 us -> 58.7 us
  local copies, waits for them, and re-layouts: 47.9 us -> 14.6 us
  between operations: 15.1 us -> 1.51 us
    psum x4 -> x0, waiting for transfers between devices: 661 us -> none  [spread_2(): return lax.psum(kept, axis)]
    all_to_all x2 -> x3, waiting for transfers between devices: 383 us -> 169 us  [the longest x1 95.3 us: shards(): lax.all_to_all(outgoing, 'prow', split_axis=0, concat_axis=0, tiled=True)]
    pallas_call x0 -> x6, Pallas kernels: none -> 186 us  [the longest x1 79.6 us: share(): pl.pallas_call(share_kernel, out_shape=(jax.ShapeDtypeStruct((count, rows...]
    dot_general x7 -> x3, matrix products: 74.4 us -> 7 us  [the longest x1 2.64 us: shards(): lax.dot_general(left, right, (((1,), (0,)), ((), ())), precision=high)]
    all_to_all x2 -> x3, starting transfers between devices: 15.6 us -> 58.7 us  [the longest x1 48.3 us: shards(): lax.all_to_all(outgoing, 'prow', split_axis=0, concat_axis=0, tiled=True)]
    dot_general x2 -> x1, local copies, waits for them, and re-layouts: 18.7 us -> 1.15 us  [shards(): lax.dot_general(row_raw, inverse, (((1,), (1,)), ((), ())), precision=high)]
    another operation x11 -> x10, other arithmetic: 54.1 us -> 54.6 us  [the longest x7 34.7 us: shards(): factor = jnp.linalg.cholesky(pivot)]
  transfers between devices with their start and end apart: 6 -> 3, of which waited for: 6 -> 3; matrix products, arithmetic and copies ran while one was open for 1% -> 1% of each run, Pallas kernels for 0% -> 0%
where the time goes in v1:
time: 501 us; the launch traced here: 500 us
  Pallas kernels  186 us (37%)
  waiting for transfers between devices  169 us (34%)
  other arithmetic  60.8 us (12%)
  starting transfers between devices  58.7 us (12%)
  local copies, waits for them, and re-layouts  14.6 us (3%)
  matrix products  8.42 us (2%)
    all_to_all x1, waiting for transfers between devices, shards(): lax.all_to_all(outgoing, 'prow', split_axis=0, concat_axis=0, tiled=True)  95.3 us
    pallas_call x1, Pallas kernels, share(): pl.pallas_call(share_kernel, out_shape=(jax.ShapeDtypeStruct((count, rows...  79.6 us
    all_to_all x1, waiting for transfers between devices, shards(): lax.all_to_all(dealt, ('half', 'pcol'), split_axis=0, concat_axis=0, tile...  72.3 us
    pallas_call x1, Pallas kernels, spread(): pl.pallas_call(spread_kernel, out_shape=jax.ShapeDtypeStruct((2, rows, co...  72.1 us
    all_to_all x1, starting transfers between devices, shards(): lax.all_to_all(outgoing, 'prow', split_axis=0, concat_axis=0, tiled=True)  48.3 us
    another operation x7, other arithmetic, shards(): factor = jnp.linalg.cholesky(pivot)  34.7 us
    another operation x3, other arithmetic, shards(): lax.linalg.triangular_solve(factor, jnp.eye(RP, dtype=jnp.float32), left_...  19.9 us
    pallas_call x1, Pallas kernels, pick(): pl.pallas_call(pick_kernel, out_shape=jax.ShapeDtypeStruct((count,) + sou...  10.4 us
  transfers between devices with their start and end apart: 3, of which 3 were waited for; matrix products, arithmetic and copies ran while one was open for 1% of the time, Pallas kernels for 0%

profile of v1, /device:TPU:4, one launch (start us, length us, event | category | flops | bytes accessed | tf_op | source)
XLA Modules:
  0.0 499.8 jit_solution(10069307232372480843)
XLA Ops:
  0.0 72.1 %shard_map.46 = f32[2,512,1024]{2,1,0:T(8,128)} custom-call(f32[512,1024]{1,0:T(8,128)} %bitcast.42), custom_call_target="tpu_custom_call" | custom-call | tf_op jit(solution)/shard_map/pallas_call | solution.py:130
  72.1 8.3 %shard_map.47 = f32[2,4,64,1024]{3,2,1,0:T(8,128)} custom-call(f32[512,1024]{1,0:T(8,128)} %bitcast.43, f32[1024,1024]{1,0:T(8,128)} %bitcast.41, f32[512,1024]{1,0:T(8,128)} %bitcast.45), custom_call_target="tpu_custom_call" | custom-call | tf_op jit(solution)/shard_map/pallas_call | solution.py:169
  80.4 0.0 copy-start.3
  80.4 3.9 all-to-all-start
  84.3 0.0 copy-done.3
  84.3 0.1 compare_and_fusion
  84.4 0.1 fusion.15
  84.5 0.1 and.44
  84.6 0.1 div.47
  84.7 0.6 select_reduce_fusion.3.index
  85.3 1.9 all-to-all-done
  87.2 0.0 copy-start.1
  87.2 1.3 copy-done.1
  88.5 10.4 %shard_map.48 = f32[16,64,1024]{2,1,0:T(8,128)} custom-call(s32[16]{0:T(128)} %select_reduce_fusion.3.index, f32[8,64,1024]{2,1,0:T(8,128)} %bitcast.44), custom_call_target="tpu_custom_call" | custom-call | tf_op jit(solution)/shard_map/pallas_call | solution.py:189
  98.9 48.3 %all-to-all-start.1 = ((f32[16,64,1024]{2,1,0:T(8,128)}), f32[16,64,1024]{2,1,0:T(8,128)}, u32[]{:S(2)}, u32[]{:S(2)}) async-start(f32[16,64,1024]{2,1,0:T(8,128)} %shard_map.48), calls=%async_computation.1 | async-start | bytes 8388608 | tf_op jit(solution)/shard_map/all_to_all | solution.py:472
  147.3 0.3 fusion.12
  147.6 0.7 copy.16.rows
  148.3 0.1 and_select_fusion
  148.4 0.7 select_reduce_fusion.2.cols
  149.0 95.3 %all-to-all-done.1.arrived = f32[16,64,1024]{2,1,0:T(8,128)} async-done(((f32[16,64,1024]{2,1,0:T(8,128)}), f32[16,64,1024]{2,1,0:T(8,128)}, u32[]{:S(2)}, u32[]{:S(2)}) %all-to-all-start.1) | async-done | bytes 4194336 | tf_op jit(solution)/shard_map/all_to_all | solution.py:472
  244.3 9.3 %shard_map.49 = f32[16,2,6,64,128]{4,3,2,1,0:T(8,128)} custom-call(s32[2,6]{1,0:T(2,128)} %copy.16.rows, s32[2,16]{1,0:T(2,128)} %select_reduce_fusion.2.cols, f32[16,64,1024]{2,1,0:T(8,128)} %all-to-all-done.1.arrived), custom_call_target="tpu_custom_call" | custom-call | tf_op jit(solution)/shard_map/pallas_call | solution.py:210
  253.7 6.5 %all-to-all-start.2 = ((f32[16,2,6,64,128]{4,3,2,1,0:T(8,128)}), f32[16,2,6,64,128]{4,3,2,1,0:T(8,128)}, u32[]{:S(2)}, u32[]{:S(2)}) async-start(f32[16,2,6,64,128]{4,3,2,1,0:T(8,128)} %shard_map.49), calls=%async_computation.2 | async-start | bytes 12582912 | tf_op jit(solution)/shard_map/all_to_all | solution.py:474
  260.2 0.7 copy.17.source
  260.8 0.4 compare_reduce_fusion.1
  261.2 0.1 copy.23
  261.3 0.6 convert_element_type.9.row_there
  261.9 0.1 copy.24
  262.0 0.6 convert_element_type.10.col_there
  262.6 72.3 %all-to-all-done.2.refs_0_.refs_1_.refs_2_.refs_3_ = f32[16,2,6,64,128]{4,3,2,1,0:T(8,128)} async-done(((f32[16,2,6,64,128]{4,3,2,1,0:T(8,128)}), f32[16,2,6,64,128]{4,3,2,1,0:T(8,128)}, u32[]{:S(2)}, u32[]{:S(2)}) %all-to-all-start.2) | async-done | bytes 6291488 | tf_op jit(solution)/shard_map/all_to_all | solution.py:474
  334.9 6.5 %shard_map.50 = f32[768,768]{1,0:T(8,128)} custom-call(s32[2,6]{1,0:T(2,128)} %copy.17.source, s32[2,6]{1,0:T(2,128)} %convert_element_type.9.row_there, s32[2,6]{1,0:T(2,128)} %convert_element_type.10.col_there, f32[768,768]{1,0:T(8,128)} %root.1, f32[16,2,6,64,128]{4,3,2,1,0:T(8,128)} %all-to-all-done.2.refs_0_.refs_1_.refs_2_.refs_3_, ...), custom_call_target="tpu_custom_call" | custom-call | tf_op jit(solution)/shard_map/pallas_call | solution.py:249
  341.4 2.1 slice.70.row_raw
  343.5 2.1 slice.71.col_raw
  345.6 79.6 %shard_map.51 = (f32[16,48,256]{2,1,0:T(8,128)}, f32[16,16,768]{2,1,0:T(8,128)}, f32[16,16,256]{2,1,0:T(8,128)}) custom-call(f32[768,256]{1,0:T(8,128)} %slice.70.row_raw, f32[256,768]{1,0:T(8,128)} %slice.71.col_raw), custom_call_target="tpu_custom_call" | custom-call | tf_op jit(solution)/shard_map/pallas_call | solution.py:422
  425.2 1.1 copy.18
  426.3 1.0 fusion
  427.3 11.7 %cholesky.50 = f32[128,128]{1,0:T(8,128)S(1)} custom-call(f32[128,128]{1,0:T(8,128)S(1)} %cholesky.118), custom_call_target="Cholesky" | custom-call | tf_op jit(solution)/shard_map/jit(cholesky)/cholesky | solution.py:480
  439.0 9.8 %custom-call.14 = f32[1,128,128]{1,2,0:T(8,128)S(1)} custom-call(f32[1,128,128]{2,1,0:T(8,128)S(1)} %get-tuple-element.38), custom_call_target="InvertDiagBlocksLowerTriangular" | custom-call | tf_op jit(solution)/shard_map/jit(cholesky)/cholesky | solution.py:480
  448.9 0.3 fusion.8
  449.2 0.3 convolution_subtract_fusion.1
  449.4 0.1 copy.19
  449.5 11.7 %cholesky.105 = f32[128,128]{1,0:T(8,128)S(1)} custom-call(f32[128,128]{1,0:T(8,128)S(1)} %convolution_subtract_fusion.1), custom_call_target="Cholesky" | custom-call | tf_op jit(solution)/shard_map/jit(cholesky)/cholesky | solution.py:480
  461.3 0.7 compare_reduce_fusion.3
  462.0 0.7 compare_reduce_fusion.2
  464.0 0.1 triangular_solve.44
  464.1 3.9 while.1
  464.1 0.6 fusion.28
  464.7 1.3 bitcast_dynamic-update-slice_fusion.2
  466.0 0.6 fusion.28
  466.7 1.3 bitcast_dynamic-update-slice_fusion.2
  468.0 19.9 %custom-call.15 = f32[2,128,128]{1,2,0:T(8,128)S(1)} custom-call(f32[2,128,128]{2,1,0:T(8,128)S(1)} %get-tuple-element.18), custom_call_target="InvertDiagBlocksLowerTriangular" | custom-call | tf_op jit(solution)/shard_map/triangular_solve | solution.py:481
  487.9 0.3 fusion.4
  488.2 0.3 convolution_subtract_fusion
  488.5 0.3 fusion.7
  488.8 0.0 copy-start
  488.8 1.8 fusion.3
  490.6 2.6 fusion.2
  493.1 1.1 copy.20
  494.3 0.0 copy-done
  494.3 2.6 select_subtract_fusion
  496.9 0.0 copy-start.2
  497.0 0.2 slice.73
  497.2 0.9 copy-done.2
  498.1 0.2 slice_select_fusion
  498.3 1.6 pad_maximum_fusion
  (16 shorter events, 0.2 us)
Async XLA Ops:
  80.4 3.9 copy-start.3
  80.4 6.8 %all-to-all-start = ((f32[2,4,64,1024]{3,2,1,0:T(8,128)}), f32[2,4,64,1024]{3,2,1,0:T(8,128)S(1)}, u32[]{:S(2)}, u32[]{:S(2)}) async-start(f32[2,4,64,1024]{3,2,1,0:T(8,128)} %shard_map.47), calls=%async_computation | async-start | bytes 4194304 | tf_op jit(solution)/shard_map/all_to_all | solution.py:470
  87.2 1.3 copy-start.1
  98.9 145.4 %all-to-all-start.1 = ((f32[16,64,1024]{2,1,0:T(8,128)}), f32[16,64,1024]{2,1,0:T(8,128)}, u32[]{:S(2)}, u32[]{:S(2)}) async-start(f32[16,64,1024]{2,1,0:T(8,128)} %shard_map.48), calls=%async_computation.1 | async-start | bytes 8388608 | tf_op jit(solution)/shard_map/all_to_all | solution.py:472
  253.7 81.2 %all-to-all-start.2 = ((f32[16,2,6,64,128]{4,3,2,1,0:T(8,128)}), f32[16,2,6,64,128]{4,3,2,1,0:T(8,128)}, u32[]{:S(2)}, u32[]{:S(2)}) async-start(f32[16,2,6,64,128]{4,3,2,1,0:T(8,128)} %shard_map.49), calls=%async_computation.2 | async-start | bytes 12582912 | tf_op jit(solution)/shard_map/all_to_all | solution.py:474
  488.8 5.5 %copy-start = (f32[768,768]{1,0:T(8,128)S(1)}, f32[768,768]{1,0:T(8,128)}, u32[]{:S(2)}) copy-start(f32[768,768]{1,0:T(8,128)} %shard_map.50) | copy-start | bytes 7077892
  496.9 1.1 copy-start.2

commit v2 on v1

v2 whole, which is shorter than its diff:
```python
import functools

import jax
import jax.numpy as jnp
from jax import lax
from jax.experimental import pallas as pl
from jax.experimental.pallas import tpu as pltpu
from jax.sharding import PartitionSpec as P

BLK = 128
RP = 256
HALF = BLK // 2
NZ = 8
CHUNKS = 32
TILE = 256
MESH = pl.DeviceIdType.MESH
ANY = pl.BlockSpec(memory_space=pl.ANY)


def position():
    return lax.axis_index("half"), lax.axis_index("prow"), lax.axis_index("pcol")


def greet(devices):
    barrier = pltpu.get_barrier_semaphore()
    for device in devices:
        pl.semaphore_signal(barrier, inc=1, device_id=device, device_id_type=MESH)
    pl.semaphore_wait(barrier, len(devices))


def split(value):
    high = value.astype(jnp.bfloat16)
    return high, (value - high.astype(jnp.float32)).astype(jnp.bfloat16)


def dot3(left, right, dims):
    dot = functools.partial(
        lax.dot_general, dimension_numbers=(dims, ((), ())), preferred_element_type=jnp.float32)
    return dot(left[0], right[0]) + (dot(left[0], right[1]) + dot(left[1], right[0]))


def spread_kernel(leaves, panel, update, outgoing, cols, through, high, low, both, away,
                  ring_send, ring_recv, hand_send, hand_recv, side_send, swap_send, swap_recv):
    core, prow, pcol = position()
    z, x = prow // 2, prow % 2
    partner = (1 - core, prow, pcol)
    upper = (core, ((z + 1) % NZ) * 2 + x, pcol)
    lower = (core, ((z + NZ - 1) % NZ) * 2 + x, pcol)
    beside = z * 2 + (1 - x)
    across = (pcol + 4) % 8
    greet((upper, lower, partner, (0, beside, across), (1, beside, across)))
    ahead = (core, ((z + 1 + (NZ - 2) * core) % NZ) * 2 + x, pcol)
    size = panel.shape[0]
    rows = size // CHUNKS
    above = (z + NZ - pcol) % NZ
    far = jnp.where(core == 0, above, (pcol + NZ - z) % NZ)
    which = jnp.where(core == 0, x, 1 - x)
    at_source = above == 0
    from_side = z == across

    def piece(index):
        return pl.ds(pl.multiple_of(index * rows, rows), rows)

    def own_ring(index, source):
        return pltpu.make_async_remote_copy(
            source, cols.at[which, piece(index)], ring_send.at[0, index],
            ring_recv.at[core, index], device_id=ahead, device_id_type=MESH)

    def pass_ring(index):
        return pltpu.make_async_remote_copy(
            through.at[piece(index)], through.at[piece(index)], ring_send.at[1, index],
            ring_recv.at[1 - core, index], device_id=ahead, device_id_type=MESH)

    def hand(index):
        return pltpu.make_async_remote_copy(
            through.at[piece(index)], cols.at[which, piece(index)], hand_send.at[index],
            hand_recv.at[index], device_id=partner, device_id_type=MESH)

    def feed(index):
        return pltpu.make_async_remote_copy(
            panel.at[piece(index)], through.at[piece(index)], side_send.at[index],
            ring_recv.at[1, index], device_id=(0, prow, pcol), device_id_type=MESH)

    def side_own(index):
        return pltpu.make_async_remote_copy(
            panel.at[piece(index)], cols.at[x, piece(index)], side_send.at[index],
            ring_recv.at[1, index], device_id=(1, beside, across), device_id_type=MESH)

    def side_pass(index):
        return pltpu.make_async_remote_copy(
            panel.at[piece(index)], through.at[piece(index)], side_send.at[index],
            ring_recv.at[0, index], device_id=(1, beside, across), device_id_type=MESH)

    def each(body):
        @pl.loop(0, CHUNKS)
        def _(index):
            body(index)

    @pl.when(from_side & (core == 1))
    def _():
        each(lambda index: side_own(index).start())

    @pl.when(from_side & (core == 0))
    def _():
        each(lambda index: side_pass(index).start())

    @pl.when(at_source & (core == 1))
    def _():
        each(lambda index: feed(index).start())

    head = at_source & (core == 0)
    last = far == NZ - 1

    @pl.loop(0, CHUNKS)
    def _(index):
        here = piece(index)

        @pl.when(head)
        def _():
            own_ring(index, panel.at[here]).start()

        @pl.when(jnp.logical_not(head))
        def _():
            copy = own_ring(index, cols.at[which, here])
            copy.wait_recv()

            @pl.when(jnp.logical_not(last))
            def _():
                copy.start()

        copy = pass_ring(index)
        copy.wait_recv()

        @pl.when(jnp.logical_not(last))
        def _():
            copy.start()

        @pl.when(jnp.logical_not(head))
        def _():
            hand(index).start()

    @pl.when(at_source)
    def _():
        cols[x] = panel[...]

    high[...], low[...] = split(panel[...])

    def multiply(tile):
        columns = cols[tile * TILE // size, pl.ds(tile * TILE % size, TILE)]
        product = dot3((high[...], low[...]), split(columns), ((1,), (1,)))
        place = pl.ds(tile * TILE, TILE)
        value = update[:, place] - product
        for block in range(size // BLK):
            top = value[block * BLK : block * BLK + HALF]
            bottom = value[block * BLK + HALF : (block + 1) * BLK]
            both[core, block, :, place] = jnp.where(core == 0, top, bottom)
            away[block, :, place] = jnp.where(core == 0, bottom, top)

    @pl.when(jnp.logical_not(at_source & (core == 1)))
    def _():
        def arrive(index):
            pltpu.make_async_remote_copy(
                through.at[piece(index)], cols.at[1 - which, piece(index)], hand_send.at[index],
                hand_recv.at[index], device_id=partner, device_id_type=MESH).wait_recv()

        each(arrive)

    for tile in range(2 * size // TILE):
        multiply(tile)
    swap = pltpu.make_async_remote_copy(
        away, both.at[core], swap_send, swap_recv, device_id=partner, device_id_type=MESH)
    swap.start()

    @pl.when(jnp.logical_not(last))
    def _():
        each(lambda index: own_ring(index, panel.at[piece(index)]).wait_send())
        each(lambda index: pass_ring(index).wait_send())

    @pl.when(jnp.logical_not(head))
    def _():
        each(lambda index: hand(index).wait_send())

    @pl.when(from_side | (at_source & (core == 1)))
    def _():
        each(lambda index: feed(index).wait_send())

    swap.wait_send()
    pltpu.make_async_remote_copy(
        away, both.at[1 - core], swap_send, swap_recv, device_id=partner,
        device_id_type=MESH).wait_recv()
    for target in range(outgoing.shape[0]):
        leaf = leaves[target]
        outgoing[target] = both[leaf // 4, leaf % 4]


def spread(leaves, panel, update):
    rows, depth = panel.shape
    width = update.shape[1]
    blocks = rows // BLK
    sems = pltpu.SemaphoreType.DMA((CHUNKS,))
    vmem = pl.BlockSpec(memory_space=pltpu.VMEM)
    return pl.pallas_call(
        spread_kernel,
        out_shape=jax.ShapeDtypeStruct((leaves.shape[0], HALF, width), jnp.float32),
        in_specs=[pl.BlockSpec(memory_space=pltpu.SMEM), vmem, vmem],
        out_specs=vmem,
        scratch_shapes=[
            pltpu.VMEM((2, rows, depth), jnp.float32),
            pltpu.VMEM((rows, depth), jnp.float32),
            pltpu.VMEM((rows, depth), jnp.bfloat16),
            pltpu.VMEM((rows, depth), jnp.bfloat16),
            pltpu.VMEM((2, blocks, HALF, width), jnp.float32),
            pltpu.VMEM((blocks, HALF, width), jnp.float32),
        ] + [pltpu.SemaphoreType.DMA((2, CHUNKS))] * 2 + [sems] * 3
        + [pltpu.SemaphoreType.DMA] * 2,
        compiler_params=pltpu.CompilerParams(collective_id=0, has_side_effects=True),
    )(leaves, panel, update)


def deal_kernel(rows, cols, arrived, out):
    child = pl.program_id(0)
    for group in range(out.shape[0]):
        start = pl.multiple_of(cols[child, group] * BLK, BLK)
        out[group, 0, 0] = arrived[0, :, pl.ds(start, BLK)]


def deal(rows, cols, arrived, groups, slots):
    width = arrived.shape[2]
    return pl.pallas_call(
        deal_kernel,
        out_shape=jax.ShapeDtypeStruct((groups, 2, slots, HALF, BLK), jnp.float32),
        grid_spec=pltpu.PrefetchScalarGridSpec(
            num_scalar_prefetch=2,
            grid=(2, slots),
            in_specs=[
                pl.BlockSpec((1, HALF, width), lambda c, i, rows, cols: (rows[c, i], 0, 0))],
            out_specs=pl.BlockSpec(
                (groups, 1, 1, HALF, BLK), lambda c, i, rows, cols: (0, c, i, 0, 0)),
        ),
    )(rows, cols, arrived)


def extend_kernel(source, row_there, col_there, root, *refs):
    parts, (out, row_raw, col_raw) = refs[:4], refs[4:]
    column = pl.program_id(0)
    for slot in range(out.shape[0] // BLK):
        for half in range(2):
            rows = pl.ds(slot * BLK + half * HALF, HALF)
            value = root[rows, :]
            for child in range(2):
                there = row_there[child, slot] * col_there[child, column] > 0
                part = parts[child * 2 + half][0, 0, slot]
                value = value + jnp.where(there, part, 0.0)
            out[rows, :] = value
            if slot < RP // BLK:
                col_raw[rows, :] = value

    @pl.when(column < RP // BLK)
    def _():
        row_raw[...] = out[...]


def extend(source, row_there, col_there, root, incoming):
    rows, cols = root.shape
    slots = cols // BLK
    groups = incoming.shape[0] // 2

    def part(child, half):
        return pl.BlockSpec(
            (1, 1, rows // BLK, HALF, BLK),
            lambda j, source, *_: (half * groups + source[child, j], child, 0, 0, 0))

    column = pl.BlockSpec((rows, BLK), lambda j, *_: (0, j))
    return pl.pallas_call(
        extend_kernel,
        out_shape=(jax.ShapeDtypeStruct(root.shape, jnp.float32),
                   jax.ShapeDtypeStruct((rows, RP), jnp.float32),
                   jax.ShapeDtypeStruct((RP, cols), jnp.float32)),
        grid_spec=pltpu.PrefetchScalarGridSpec(
            num_scalar_prefetch=3,
            grid=(slots,),
            in_specs=[column] + [part(c, h) for c in range(2) for h in range(2)],
            out_specs=(column,
                       pl.BlockSpec((rows, BLK), lambda j, *_: (0, jnp.minimum(j, RP // BLK - 1))),
                       pl.BlockSpec((RP, BLK), lambda j, *_: (0, j))),
        ),
    )(source, row_there, col_there, root, *[incoming] * 4)


def remote(source, target, send, recv, device):
    return pltpu.make_async_remote_copy(
        source, target, send, recv, device_id=device, device_id_type=MESH)


def others(me, count, body):
    @pl.loop(1, count)
    def _(step):
        body((me + step) % count)


def neighbours():
    half, prow, pcol = position()

    def in_row(k):
        return (k // 8, prow, k % 8)

    def in_col(k):
        return (half, k, pcol)

    return half * 8 + pcol, prow, in_row, in_col


def pivot_kernel(share, out, first, mid, second, first_send, first_recv, second_send,
                 second_recv, third_send, third_recv):
    count = 16
    group, prow, in_row, in_col = neighbours()
    greet([in_row((group + k) % count) for k in range(1, count)]
          + [in_col((prow + k) % count) for k in range(1, count)])

    def scatter(k):
        return remote(share.at[k], first.at[group], first_send.at[k], first_recv.at[group],
                      in_row(k))

    def across(k):
        return remote(mid, second.at[prow], second_send.at[k], second_recv.at[prow], in_col(k))

    def gather(k):
        return remote(out.at[group], out.at[group], third_send.at[k], third_recv.at[group],
                      in_row(k))

    def arrive(target, recv, k):
        remote(target.at[k], target.at[k], recv.at[k], recv.at[k], in_row((group + 1) % count)).wait_recv()

    others(group, count, lambda k: scatter(k).start())
    first[group] = share[group]
    others(group, count, lambda k: arrive(first, first_recv, k))
    total = first[0]
    for k in range(1, count):
        total = total + first[k]
    mid[...] = total
    second[prow] = total
    others(prow, count, lambda k: across(k).start())
    others(prow, count, lambda k: arrive(second, second_recv, k))
    total = second[0]
    for k in range(1, count):
        total = total + second[k]
    out[group] = total
    others(group, count, lambda k: gather(k).start())
    others(group, count, lambda k: arrive(out, third_recv, k))
    others(group, count, lambda k: scatter(k).wait_send())
    others(prow, count, lambda k: across(k).wait_send())
    others(group, count, lambda k: gather(k).wait_send())


def pivot_sum(share):
    count = 16
    rows = RP // count
    many = pltpu.SemaphoreType.DMA((count,))
    vmem = pl.BlockSpec(memory_space=pltpu.VMEM)
    pieces = pltpu.VMEM((count, rows, RP), jnp.float32)
    return pl.pallas_call(
        pivot_kernel,
        out_shape=jax.ShapeDtypeStruct((count, rows, RP), jnp.float32),
        in_specs=[vmem],
        out_specs=vmem,
        scratch_shapes=[pieces, pltpu.VMEM((rows, RP), jnp.float32), pieces] + [many] * 6,
        compiler_params=pltpu.CompilerParams(collective_id=2, has_side_effects=True),
    )(share.reshape(count, rows, RP)).reshape(RP, RP)


def share_kernel(row_raw, col_raw, row_out, col_out, row_cast, row_in, row_send, row_recv,
                 col_cast, col_in, col_send, col_recv):
    count = 16
    group, prow, in_row, in_col = neighbours()
    greet([in_row((group + k) % count) for k in range(1, count)]
          + [in_col((prow + k) % count) for k in range(1, count)])

    def row_first(k):
        return remote(row_raw.at[k], row_out.at[k], row_cast.at[k], row_in, in_row(k))

    def row_second(k):
        return remote(row_out.at[group], row_out.at[group], row_send.at[k], row_recv.at[group],
                      in_row(k))

    def col_first(k):
        return remote(col_raw.at[k], col_out.at[k], col_cast.at[k], col_in, in_col(k))

    def col_second(k):
        return remote(col_out.at[prow], col_out.at[prow], col_send.at[k], col_recv.at[prow],
                      in_col(k))

    def row_start(k):
        return remote(row_raw.at[0], row_out.at[0], row_send.at[k], row_recv.at[0], in_row(k))

    def col_start(k):
        return remote(col_raw.at[0], col_out.at[0], col_send.at[k], col_recv.at[0], in_col(k))

    def spare_first(k, body):
        @pl.when(k > 0)
        def _():
            body()

    @pl.when(group == 0)
    def _():
        others(group, count, lambda k: row_first(k).start())

    @pl.when(prow == 0)
    def _():
        others(prow, count, lambda k: col_first(k).start())

    @pl.when(group == 0)
    def _():
        others(group, count, lambda k: row_start(k).start())
        row_out[...] = row_raw[...]

    @pl.when(prow == 0)
    def _():
        others(prow, count, lambda k: col_start(k).start())
        col_out[...] = col_raw[...]

    @pl.when(group > 0)
    def _():
        row_first(group).wait_recv()
        others(group, count, lambda k: spare_first(k, lambda: row_second(k).start()))

    @pl.when(prow > 0)
    def _():
        col_first(prow).wait_recv()
        others(prow, count, lambda k: spare_first(k, lambda: col_second(k).start()))

    def arrive(target, recv, k):
        remote(target.at[k], target.at[k], recv.at[k], recv.at[k], in_row((group + 1) % count)).wait_recv()

    @pl.when(group > 0)
    def _():
        others(group, count, lambda k: arrive(row_out, row_recv, k))

    @pl.when(prow > 0)
    def _():
        others(prow, count, lambda k: arrive(col_out, col_recv, k))

    @pl.when(group == 0)
    def _():
        others(group, count, lambda k: row_first(k).wait_send())

    @pl.when(prow == 0)
    def _():
        others(prow, count, lambda k: col_first(k).wait_send())

    others(group, count, lambda k: spare_first(k, lambda: row_second(k).wait_send()))
    others(prow, count, lambda k: spare_first(k, lambda: col_second(k).wait_send()))


def share(row_raw, col_raw):
    count = 16
    one, many = pltpu.SemaphoreType.DMA, pltpu.SemaphoreType.DMA((count,))
    vmem = pl.BlockSpec(memory_space=pltpu.VMEM)
    rows, cols = row_raw.shape[0], col_raw.shape[1]
    row_shape = (count, rows // count, RP)
    col_shape = (count, RP // count, cols)
    row_out, col_out = pl.pallas_call(
        share_kernel,
        out_shape=(jax.ShapeDtypeStruct(row_shape, jnp.float32),
                   jax.ShapeDtypeStruct(col_shape, jnp.float32)),
        in_specs=[vmem, vmem],
        out_specs=(vmem, vmem),
        scratch_shapes=[many, one, many, many, many, one, many, many],
        compiler_params=pltpu.CompilerParams(collective_id=1, has_side_effects=True),
    )(row_raw.reshape(row_shape), col_raw.reshape(col_shape))
    return row_out.reshape(rows, RP), col_out.reshape(RP, cols)


def find(labels, wanted, values):
    hit = labels[..., None, :] == wanted[:, None]
    return jnp.sum(jnp.where(hit, values, 0), axis=-1).astype(jnp.int32), jnp.any(hit, axis=-1)


def shards(child_update, child_panel, root_front, index_map):
    rows_dev, cols_dev = child_update.shape[1:]
    root_rows, root_cols = root_front.shape
    row_count, col_count, groups = 16, 8, 16
    row_index = lax.axis_index("prow")
    col_index = lax.axis_index("pcol")
    group_index = lax.axis_index(("half", "pcol"))
    row_slots, col_slots = root_rows // BLK, root_cols // BLK
    child_blocks, col_blocks = rows_dev // BLK, cols_dev // BLK
    blocks = jnp.arange(index_map.shape[1], dtype=jnp.int32)
    everyone = jnp.arange(row_count, dtype=jnp.int32)

    own_rows = lax.dynamic_slice_in_dim(index_map, row_index * child_blocks, child_blocks, 1)
    leaves, _ = find(own_rows.reshape(-1) // row_slots, everyone,
                     jnp.arange(2 * child_blocks, dtype=jnp.int32))
    row_source, row_there = find(
        index_map, row_index * row_slots + jnp.arange(row_slots, dtype=jnp.int32),
        blocks // child_blocks)
    own_cols = lax.dynamic_slice_in_dim(index_map, col_index * col_blocks, col_blocks, 1)
    col_leaves, _ = find(own_cols // col_slots, everyone, jnp.arange(col_blocks, dtype=jnp.int32))
    col_source, col_there = find(
        index_map, group_index * col_slots + jnp.arange(col_slots, dtype=jnp.int32),
        blocks // col_blocks)

    outgoing = spread(leaves, child_panel[0], child_update[0])
    arrived = lax.all_to_all(outgoing, "prow", split_axis=0, concat_axis=0, tiled=True)

    lead = own_rows.reshape(-1)
    lead_hit = lead < RP // BLK
    lead_row = jnp.sum(jnp.where(lead_hit, lead, 0))
    lead_child = jnp.sum(jnp.where(lead_hit, jnp.arange(lead.shape[0]) // child_blocks, 0))
    lead_cols = lax.dynamic_index_in_dim(own_cols, lead_child, 0, keepdims=False)
    col_hit = lead_cols < RP // BLK
    lead_col = jnp.sum(jnp.where(col_hit, lead_cols, 0))
    lead_start = jnp.sum(jnp.where(col_hit, jnp.arange(col_blocks) * BLK, 0))
    lead_block = lax.dynamic_slice(outgoing, (0, 0, lead_start), (1, HALF, BLK))[0]
    lead_block = jnp.where(jnp.any(lead_hit) & jnp.any(col_hit), lead_block, 0.0)
    lead_root = jnp.where((row_index == 0) & (group_index == 0), root_front[:RP, :RP], 0.0)
    at = (lead_row * BLK + lax.axis_index("half") * HALF, lead_col * BLK)
    lead_part = lax.dynamic_update_slice(
        lead_root, lead_block + lax.dynamic_slice(lead_root, at, (HALF, BLK)), at)
    pivot, arrived = lax.optimization_barrier((pivot_sum(lead_part), arrived))
    factor = jnp.linalg.cholesky(pivot)
    inverse = lax.linalg.triangular_solve(
        factor, jnp.eye(RP, dtype=jnp.float32), left_side=True, lower=True)

    dealt = deal(row_source, col_leaves, arrived, groups, row_slots)
    incoming = lax.all_to_all(dealt, ("half", "pcol"), split_axis=0, concat_axis=0, tiled=True)
    assembled, row_raw, col_raw = extend(
        col_source, row_there.astype(jnp.int32), col_there.astype(jnp.int32), root_front, incoming)
    row_raw, col_raw = share(row_raw, col_raw)

    high = lax.Precision.HIGH
    global_rows = row_index * root_rows + jnp.arange(root_rows, dtype=jnp.int32)
    global_cols = group_index * root_cols + jnp.arange(root_cols, dtype=jnp.int32)
    left = lax.dot_general(row_raw, inverse, (((1,), (1,)), ((), ())), precision=high)
    right = lax.dot_general(inverse, col_raw, (((1,), (0,)), ((), ())), precision=high)
    update = lax.dot_general(left, right, (((1,), (0,)), ((), ())), precision=high)
    trailing_mask = (global_rows[:, None] >= RP) & (global_cols[None, :] >= RP)
    trailing = assembled - jnp.where(trailing_mask, update, 0.0)
    leading = jnp.pad(factor, ((0, root_rows - RP), (0, 0)))
    panel = jnp.where(global_rows[:, None] < RP, leading, left)
    panel_cols = jnp.where(group_index == 0, panel, trailing[:, :RP])
    return jnp.concatenate([panel_cols, trailing[:, RP:]], axis=1)


def solution(mesh):
    return jax.shard_map(
        shards,
        mesh=mesh,
        in_specs=(
            P("half", "prow", "pcol"),
            P("half", "prow", None),
            P("prow", ("half", "pcol")),
            P(),
        ),
        out_specs=P("prow", ("half", "pcol")),
        check_vma=False,
    )
```

time: 501 us -> 357 us (0.71)
  waiting for transfers between devices: 169 us -> 11.1 us
  Pallas kernels: 186 us -> 224 us
  starting transfers between devices: 58.7 us -> 33.1 us
  local copies, waits for them, and re-layouts: 14.6 us -> 7.14 us
  between operations: 1.51 us -> 7.85 us
    all_to_all x1, waiting for transfers between devices: 95.3 us -> 0.01 us  [shards(): lax.all_to_all(outgoing, 'prow', split_axis=0, concat_axis=0, tiled=True)]
    all_to_all x1, waiting for transfers between devices: 72.3 us -> 11.1 us  [shards(): lax.all_to_all(dealt, ('half', 'pcol'), split_axis=0, concat_axis=0, tile...]
    pallas_call x5 -> x4, Pallas kernels: 177 us -> 215 us  [the longest x1 99.9 us: pivot_sum(): pl.pallas_call(pivot_kernel, out_shape=jax.ShapeDtypeStruct((count, rows,...]
    all_to_all x1, starting transfers between devices: 48.3 us -> 28.2 us  [shards(): lax.all_to_all(outgoing, 'prow', split_axis=0, concat_axis=0, tiled=True)]
    another operation x7 -> x6, other arithmetic: 34.7 us -> 34 us  [shards(): factor = jnp.linalg.cholesky(pivot)]
  transfers between devices with their start and end apart: 3 -> 2, of which waited for: 3 -> 1; matrix products, arithmetic and copies ran while one was open for 1% -> 19% of each run, Pallas kernels for 0% -> 28%
where the time goes in v2:
time: 357 us; the launch traced here: 355 us
  Pallas kernels  224 us (63%)
  other arithmetic  65.2 us (18%)
  starting transfers between devices  33.1 us (9%)
  waiting for transfers between devices  11.1 us (3%)
  between operations  7.85 us (2%)
  local copies, waits for them, and re-layouts  7.14 us (2%)
  matrix products  6.87 us (2%)
    pallas_call x1, Pallas kernels, pivot_sum(): pl.pallas_call(pivot_kernel, out_shape=jax.ShapeDtypeStruct((count, rows,...  99.9 us
    pallas_call x1, Pallas kernels, spread(): pl.pallas_call(spread_kernel, out_shape=jax.ShapeDtypeStruct((leaves.shap...  64.6 us
    pallas_call x1, Pallas kernels, share(): pl.pallas_call(share_kernel, out_shape=(jax.ShapeDtypeStruct(row_shape, j...  43.1 us
    another operation x6, other arithmetic, shards(): factor = jnp.linalg.cholesky(pivot)  34 us
    all_to_all x1, starting transfers between devices, shards(): lax.all_to_all(outgoing, 'prow', split_axis=0, concat_axis=0, tiled=True)  28.2 us
    another operation x3, other arithmetic, shards(): lax.linalg.triangular_solve(factor, jnp.eye(RP, dtype=jnp.float32), left_...  19.9 us
    all_to_all x1, waiting for transfers between devices, shards(): lax.all_to_all(dealt, ('half', 'pcol'), split_axis=0, concat_axis=0, tile...  11.1 us
    pallas_call x1, Pallas kernels, deal(): pl.pallas_call(deal_kernel, out_shape=jax.ShapeDtypeStruct((groups, 2, sl...  9.45 us
  transfers between devices with their start and end apart: 2, of which 1 were waited for; matrix products, arithmetic and copies ran while one was open for 19% of the time, Pallas kernels for 28%

profile of v2, /device:TPU:4, one launch (start us, length us, event | category | flops | bytes accessed | tf_op | source)
XLA Modules:
  0.0 355.5 jit_solution(1355163521216441649)
XLA Ops:
  0.0 1.4 select_reduce_fusion.5
  1.4 1.4 fusion.18
  2.8 0.1 and.56
  2.9 0.1 div.53
  3.0 0.7 select_reduce_fusion.3.leaves
  3.6 64.6 %shard_map.46 = f32[16,64,1024]{2,1,0:T(8,128)} custom-call(s32[16]{0:T(128)} %select_reduce_fusion.3.leaves, f32[512,1024]{1,0:T(8,128)} %bitcast.51, f32[512,1024]{1,0:T(8,128)} %bitcast.52), custom_call_target="tpu_custom_call" | custom-call | tf_op jit(solution)/shard_map/pallas_call | solution.py:202
  68.2 0.0 copy-start.3
  68.2 28.2 %all-to-all-start = ((f32[16,64,1024]{2,1,0:T(8,128)}), f32[16,64,1024]{2,1,0:T(8,128)}, u32[]{:S(2)}, u32[]{:S(2)}) async-start(f32[16,64,1024]{2,1,0:T(8,128)} %shard_map.46), calls=%async_computation | async-start | bytes 8388608 | tf_op jit(solution)/shard_map/all_to_all | solution.py:503
  98.8 0.0 copy-done.3
  98.8 0.8 compare_reduce_fusion.4
  99.5 0.7 fusion.16
  100.8 0.3 fusion.13
  101.2 0.7 copy.18.rows
  105.3 1.0 slice_select_fusion.1
  106.2 0.9 fusion.11
  107.2 0.0 copy-start.1
  107.2 0.7 copy-done.1
  107.9 99.9 %shard_map.47 = f32[16,16,256]{2,1,0:T(8,128)} custom-call(f32[16,16,256]{2,1,0:T(8,128)} %bitcast.53), custom_call_target="tpu_custom_call" | custom-call | tf_op jit(solution)/shard_map/pallas_call | solution.py:361
  207.8 0.1 and_select_fusion
  207.9 0.7 select_reduce_fusion.2.cols
  208.5 0.0 all-to-all-done.arrived
  208.5 9.4 %shard_map.48 = f32[16,2,6,64,128]{4,3,2,1,0:T(8,128)} custom-call(s32[2,6]{1,0:T(2,128)} %copy.18.rows, s32[2,16]{1,0:T(2,128)} %select_reduce_fusion.2.cols, f32[16,64,1024]{2,1,0:T(8,128)} %all-to-all-done.arrived), custom_call_target="tpu_custom_call" | custom-call | tf_op jit(solution)/shard_map/pallas_call | solution.py:229
  218.0 0.0 copy-start
  218.0 4.9 %all-to-all-start.1 = ((f32[16,2,6,64,128]{4,3,2,1,0:T(8,128)}), f32[16,2,6,64,128]{4,3,2,1,0:T(8,128)}, u32[]{:S(2)}, u32[]{:S(2)}) async-start(f32[16,2,6,64,128]{4,3,2,1,0:T(8,128)} %shard_map.48), calls=%async_computation.1 | async-start | bytes 12582912 | tf_op jit(solution)/shard_map/all_to_all | solution.py:525
  222.9 0.7 copy.19.source
  223.6 0.4 compare_reduce_fusion.1
  224.0 0.1 copy.23
  224.1 0.6 convert_element_type.9.row_there
  224.7 0.1 copy.24
  224.8 0.6 convert_element_type.10.col_there
  225.4 0.0 copy-done
  225.4 0.1 copy.14
  225.6 11.7 %cholesky.49 = f32[128,128]{1,0:T(8,128)S(1)} custom-call(f32[128,128]{1,0:T(8,128)S(1)} %cholesky.115), custom_call_target="Cholesky" | custom-call | tf_op jit(solution)/shard_map/jit(cholesky)/cholesky | solution.py:520
  237.4 9.8 %custom-call.14 = f32[1,128,128]{1,2,0:T(8,128)S(1)} custom-call(f32[1,128,128]{2,1,0:T(8,128)S(1)} %get-tuple-element.52), custom_call_target="InvertDiagBlocksLowerTriangular" | custom-call | tf_op jit(solution)/shard_map/jit(cholesky)/cholesky | solution.py:520
  247.2 0.3 fusion.8
  247.5 0.1 copy.15
  247.6 0.3 convolution_subtract_fusion.1
  247.9 11.7 %cholesky.103 = f32[128,128]{1,0:T(8,128)S(1)} custom-call(f32[128,128]{1,0:T(8,128)S(1)} %convolution_subtract_fusion.1), custom_call_target="Cholesky" | custom-call | tf_op jit(solution)/shard_map/jit(cholesky)/cholesky | solution.py:520
  259.7 0.7 compare_reduce_fusion.2
  261.7 0.1 triangular_solve.44
  261.7 3.9 %while.1 = (s32[]{:T(128)}, f32[256,256]{1,0:T(8,128)S(1)}, s32[2,2]{1,0:T(2,128)S(1)}, f32[2,128,128]{2,1,0:T(8,128)S(1)}, s32[]{:T(128)}) while((s32[]{:T(128)}, f32[256,256]{1,0:T(8,128)S(1)}, s32[2,2]{1,0:T(2,128)S(1)}, f32[2,128,128]{2,1,0:T(8,128)S(1)}, s32[]{:T(128)}) %tuple.35), condition=%wide.while_cond, body=%wide.while_body.sunk | while | flops 2 | bytes 131189 | solution.py:521
  261.7 0.6 fusion.31
  262.3 1.3 bitcast_dynamic-update-slice_fusion.2
  263.7 0.6 fusion.31
  264.3 1.3 bitcast_dynamic-update-slice_fusion.2
  265.6 19.9 %custom-call.15 = f32[2,128,128]{1,2,0:T(8,128)S(1)} custom-call(f32[2,128,128]{2,1,0:T(8,128)S(1)} %get-tuple-element.26), custom_call_target="InvertDiagBlocksLowerTriangular" | custom-call | tf_op jit(solution)/shard_map/triangular_solve | solution.py:521
  285.5 0.3 fusion.4
  285.8 0.3 convolution_subtract_fusion
  286.1 0.3 fusion.7
  286.4 11.1 %all-to-all-done.1.refs_0_.refs_1_.refs_2_.refs_3_ = f32[16,2,6,64,128]{4,3,2,1,0:T(8,128)} async-done(((f32[16,2,6,64,128]{4,3,2,1,0:T(8,128)}), f32[16,2,6,64,128]{4,3,2,1,0:T(8,128)}, u32[]{:S(2)}, u32[]{:S(2)}) %all-to-all-start.1) | async-done | bytes 6291488 | tf_op jit(solution)/shard_map/all_to_all | solution.py:525
  297.5 7.1 %shard_map.49 = (f32[768,768]{1,0:T(8,128)}, f32[768,256]{1,0:T(8,128)}, f32[256,768]{1,0:T(8,128)}) custom-call(s32[2,6]{1,0:T(2,128)} %copy.19.source, s32[2,6]{1,0:T(2,128)} %convert_element_type.9.row_there, s32[2,6]{1,0:T(2,128)} %convert_element_type.10.col_there, f32[768,768]{1,0:T(8,128)} %root.1, ...), custom_call_target="tpu_custom_call" | custom-call | tf_op jit(solution)/shard_map/pallas_call | solution.py:274
  304.6 43.1 %shard_map.50 = (f32[16,48,256]{2,1,0:T(8,128)}, f32[16,16,768]{2,1,0:T(8,128)}) custom-call(f32[16,48,256]{2,1,0:T(8,128)} %bitcast.56, f32[16,16,768]{2,1,0:T(8,128)} %bitcast.57), custom_call_target="tpu_custom_call" | custom-call | tf_op jit(solution)/shard_map/pallas_call | solution.py:461
  347.7 0.0 copy-start.2
  347.7 1.7 fusion.3
  349.4 0.0 copy-done.2
  349.4 0.6 fusion.2
  350.0 0.3 copy.20
  350.3 3.2 select_subtract_fusion
  353.5 0.2 slice.67
  353.7 0.2 slice_select_fusion
  353.9 1.6 pad_maximum_fusion
  (17 shorter events, 0.3 us)
Async XLA Ops:
  68.2 30.5 %copy-start.3 = (s32[2,64]{1,0:T(2,128)S(1)}, s32[2,64]{1,0:T(2,128)}, u32[]{:S(2)}) copy-start(s32[2,64]{1,0:T(2,128)} %param.7) | copy-start | bytes 1540
  68.2 140.3 %all-to-all-start = ((f32[16,64,1024]{2,1,0:T(8,128)}), f32[16,64,1024]{2,1,0:T(8,128)}, u32[]{:S(2)}, u32[]{:S(2)}) async-start(f32[16,64,1024]{2,1,0:T(8,128)} %shard_map.46), calls=%async_computation | async-start | bytes 8388608 | tf_op jit(solution)/shard_map/all_to_all | solution.py:503
  107.2 0.7 copy-start.1
  218.0 7.5 %copy-start = (f32[16,16,256]{2,1,0:T(8,128)S(1)}, f32[16,16,256]{2,1,0:T(8,128)}, u32[]{:S(2)}) copy-start(f32[16,16,256]{2,1,0:T(8,128)} %shard_map.47) | copy-start | bytes 786436
  218.0 79.5 %all-to-all-start.1 = ((f32[16,2,6,64,128]{4,3,2,1,0:T(8,128)}), f32[16,2,6,64,128]{4,3,2,1,0:T(8,128)}, u32[]{:S(2)}, u32[]{:S(2)}) async-start(f32[16,2,6,64,128]{4,3,2,1,0:T(8,128)} %shard_map.48), calls=%async_computation.1 | async-start | bytes 12582912 | tf_op jit(solution)/shard_map/all_to_all | solution.py:525
  347.7 1.7 copy-start.2

commit v3 on v2

--- a/solution.py
+++ b/solution.py
@@ -13,6 +13,10 @@
 NZ = 8
 CHUNKS = 32
 TILE = 256
+COUNT = 16
+SLOTS = 6
+PARTS = 4
+PART = HALF // PARTS
 MESH = pl.DeviceIdType.MESH
 ANY = pl.BlockSpec(memory_space=pl.ANY)
 
@@ -37,6 +41,94 @@
     dot = functools.partial(
         lax.dot_general, dimension_numbers=(dims, ((), ())), preferred_element_type=jnp.float32)
     return dot(left[0], right[0]) + (dot(left[0], right[1]) + dot(left[1], right[0]))
+
+
+def remote(source, target, send, recv, device):
+    return pltpu.make_async_remote_copy(
+        source, target, send, recv, device_id=device, device_id_type=MESH)
+
+
+def others(me, count, body):
+    @pl.loop(1, count)
+    def _(step):
+        body((me + step) % count)
+
+
+def neighbours():
+    half, prow, pcol = position()
+
+    def in_row(k):
+        return (k // 8, prow, k % 8)
+
+    def in_col(k):
+        return (half, k, pcol)
+
+    return half * 8 + pcol, prow, in_row, in_col
+
+
+def fill(table, value):
+    for i in range(table.shape[0]):
+        for j in range(table.shape[1]):
+            table[i, j] = value
+
+
+def tables_kernel(index_map, leaves, rows, cols, lead_at, source, row_there, col_there, weight):
+    group, prow, _, _ = neighbours()
+    pcol = lax.axis_index("pcol")
+    total = index_map.shape[1]
+    row_blocks, col_blocks = total // COUNT, total // 8
+    for table in (leaves, rows, cols, source, row_there, col_there):
+        fill(table, 0)
+
+    @pl.loop(0, total)
+    def _(b):
+        for child in range(2):
+            label = index_map[child, b]
+            owner = lax.div(label, SLOTS)
+            slot = label - owner * SLOTS
+
+            @pl.when(owner == prow)
+            def _():
+                rows[child, slot] = lax.div(b, row_blocks)
+                row_there[child, slot] = 1
+
+            @pl.when(owner == group)
+            def _():
+                source[child, slot] = lax.div(b, col_blocks)
+                col_there[child, slot] = 1
+
+    lead, lead_child = jnp.int32(-1), jnp.int32(0)
+    for child in range(2):
+        for b in range(row_blocks):
+            label = index_map[child, prow * row_blocks + b]
+            leaves[0, lax.div(label, SLOTS)] = child * row_blocks + b
+            lead_child = jnp.where(label < RP // BLK, child, lead_child)
+            lead = jnp.where(label < RP // BLK, label, lead)
+        for b in range(col_blocks):
+            cols[child, lax.div(index_map[child, pcol * col_blocks + b], SLOTS)] = b
+    cross, at = jnp.int32(-1), jnp.int32(0)
+    for b in range(col_blocks):
+        label = index_map[lead_child, pcol * col_blocks + b]
+        at = jnp.where(label < RP // BLK, b, at)
+        cross = jnp.where(label < RP // BLK, label, cross)
+    lead_at[0, 0] = at
+    for i in range(RP // BLK):
+        for j in range(RP // BLK):
+            hit = jnp.where((lead == i) & (cross == j), 1.0, 0.0)
+            weight[i * (RP // BLK) + j] = jnp.full(weight.shape[1:], hit, jnp.float32)
+
+
+def tables(index_map):
+    smem = pl.BlockSpec(memory_space=pltpu.SMEM)
+    vmem = pl.BlockSpec(memory_space=pltpu.VMEM)
+    shapes = [(1, COUNT), (2, SLOTS), (2, COUNT), (1, 1)] + [(2, SLOTS)] * 3
+    return pl.pallas_call(
+        tables_kernel,
+        out_shape=[jax.ShapeDtypeStruct(shape, jnp.int32) for shape in shapes]
+        + [jax.ShapeDtypeStruct(((RP // BLK) ** 2, 8, BLK), jnp.float32)],
+        in_specs=[smem],
+        out_specs=[smem] * len(shapes) + [vmem],
+    )(index_map)
 
 
 def spread_kernel(leaves, panel, update, outgoing, cols, through, high, low, both, away,
@@ -188,9 +280,14 @@
     pltpu.make_async_remote_copy(
         away, both.at[1 - core], swap_send, swap_recv, device_id=partner,
         device_id_type=MESH).wait_recv()
-    for target in range(outgoing.shape[0]):
-        leaf = leaves[target]
-        outgoing[target] = both[leaf // 4, leaf % 4]
+    blocks = size // BLK
+    for target in range(outgoing.shape[1]):
+        leaf = leaves[0, target]
+        value = both[leaf // blocks, leaf % blocks]
+        for part in range(PARTS):
+            for block in range(outgoing.shape[2]):
+                outgoing[part, target, block] = value[
+                    part * PART : (part + 1) * PART, block * BLK : (block + 1) * BLK]
 
 
 def spread(leaves, panel, update):
@@ -201,7 +298,8 @@
     vmem = pl.BlockSpec(memory_space=pltpu.VMEM)
     return pl.pallas_call(
         spread_kernel,
-        out_shape=jax.ShapeDtypeStruct((leaves.shape[0], HALF, width), jnp.float32),
+        out_shape=jax.ShapeDtypeStruct(
+            (PARTS, COUNT, width // BLK, PART, BLK), jnp.float32),
         in_specs=[pl.BlockSpec(memory_space=pltpu.SMEM), vmem, vmem],
         out_specs=vmem,
         scratch_shapes=[
@@ -217,43 +315,187 @@
     )(leaves, panel, update)
 
 
-def deal_kernel(rows, cols, arrived, out):
-    child = pl.program_id(0)
-    for group in range(out.shape[0]):
-        start = pl.multiple_of(cols[child, group] * BLK, BLK)
-        out[group, 0, 0] = arrived[0, :, pl.ds(start, BLK)]
-
-
-def deal(rows, cols, arrived, groups, slots):
-    width = arrived.shape[2]
+def eliminate(a, w):
+    size = a.shape[0]
+    lane = lax.broadcasted_iota(jnp.int32, (size, size), 1)
+    line = lax.broadcasted_iota(jnp.int32, (size, size), 0)
+    head = lax.broadcasted_iota(jnp.int32, (1, size), 1)
+    side = lax.broadcasted_iota(jnp.int32, (size, 1), 0)
+    w[...] = jnp.where(lane == line, 1.0, 0.0)
+
+    @pl.loop(0, size)
+    def _(j):
+        value = a[...]
+        column = jnp.sum(jnp.where(lane == j, value, 0.0), axis=1, keepdims=True)
+        row = a[pl.ds(j, 1), :]
+        pivot = jnp.sum(jnp.where(head == j, row, 0.0), axis=1, keepdims=True)
+        scale = 1.0 / pivot
+        column = jnp.where(side > j, column, 0.0)
+        a[...] = value - column * (row * scale)
+        w[...] = w[...] - column * (w[pl.ds(j, 1), :] * scale)
+
+    value = a[...]
+    diagonal = jnp.sum(jnp.where(lane == line, value, 0.0), axis=1, keepdims=True)
+    scale = 1.0 / jnp.sqrt(diagonal)
+    return jnp.where(lane >= line, value * scale, 0.0), w[...] * scale
+
+
+def dot_full(left, right, dims):
+    return lax.dot_general(left, right, (dims, ((), ())), precision=lax.Precision.HIGHEST,
+                           preferred_element_type=jnp.float32)
+
+
+def exchange_kernel(rows, cols, lead_at, weight, outgoing, root_pivot, incoming, factor,
+                    inverse, dealt, share, first, mid, second, pivot, a, w, row_send, row_recv,
+                    col_send, col_recv, first_send, first_recv, second_send, second_recv,
+                    third_send, third_recv, *arrived):
+    count = COUNT
+    core = lax.axis_index("half")
+    group, prow, in_row, in_col = neighbours()
+
+    def row_copy(part, k):
+        return remote(outgoing.at[part, k], arrived[part].at[prow],
+                      row_send.at[part, k], row_recv.at[part, prow], in_col(k))
+
+    def col_copy(part, k):
+        return remote(dealt.at[part, k], incoming.at[part, group], col_send.at[part, k],
+                      col_recv.at[part, group], in_row(k))
+
+    def scatter(k):
+        return remote(share.at[k], first.at[group], first_send.at[k], first_recv.at[group],
+                      in_row(k))
+
+    def across(k):
+        return remote(mid, second.at[prow], second_send.at[k], second_recv.at[prow], in_col(k))
+
+    def gather(k):
+        return remote(pivot.at[group], pivot.at[group], third_send.at[k], third_recv.at[group],
+                      in_row(k))
+
+    def row_wait(target, recv, k):
+        remote(target, target, recv, recv, in_row((group + 1) % count)).wait_recv()
+
+    def col_wait(target, recv, k):
+        remote(target, target, recv, recv, in_col((prow + 1) % count)).wait_recv()
+
+    def send_rows(part):
+        others(prow, count, lambda k: row_copy(part, k).start())
+        arrived[part][prow] = outgoing[part, prow]
+
+    def deal(part):
+        others(prow, count, lambda k: col_wait(arrived[part].at[k], row_recv.at[part, k], k))
+
+        @pl.loop(0, 2 * SLOTS)
+        def _(item):
+            child, slot = item // SLOTS, item % SLOTS
+            row = rows[child, slot]
+            for target in range(count):
+                dealt[part, target, child, slot] = arrived[part][row, cols[child, target]]
+
+        others(group, count, lambda k: col_copy(part, k).start())
+        incoming[part, group] = dealt[part, group]
+
+    greet([in_row((group + k) % count) for k in range(1, count)]
+          + [in_col((prow + k) % count) for k in range(1, count)])
+    send_rows(0)
+
+    share[...] = jnp.where((group == 0) & (prow == 0), root_pivot[...], 0.0)
+    for part in range(PARTS):
+        block = outgoing[part, 0, lead_at[0, 0]]
+        for i in range(RP // BLK):
+            line = i * (BLK // PART) + core * PARTS + part
+            for j in range(RP // BLK):
+                here = pl.ds(j * BLK, BLK)
+                scale = weight[i * (RP // BLK) + j, 0:1, :]
+                share[line, :, here] = share[line, :, here] + block * scale
+    others(group, count, lambda k: scatter(k).start())
+    first[group] = share[group]
+    others(group, count, lambda k: row_wait(first.at[k], first_recv.at[k], k))
+    value = first[0]
+    for k in range(1, count):
+        value = value + first[k]
+    mid[...] = value
+    second[prow] = value
+    others(prow, count, lambda k: across(k).start())
+    for part in range(1, PARTS):
+        send_rows(part)
+
+    others(prow, count, lambda k: col_wait(second.at[k], second_recv.at[k], k))
+    value = second[0]
+    for k in range(1, count):
+        value = value + second[k]
+    pivot[group] = value
+    others(group, count, lambda k: gather(k).start())
+    deal(0)
+    others(group, count, lambda k: row_wait(pivot.at[k], third_recv.at[k], k))
+    top, bottom = slice(0, BLK), slice(BLK, RP)
+    whole = pivot[...].reshape(RP, RP)
+    a[...] = whole[top, top]
+    upper, upper_inverse = eliminate(a, w)
+    low = dot_full(whole[bottom, top], upper_inverse, ((1,), (1,)))
+    factor[top, top] = upper.T
+    factor[top, bottom] = jnp.zeros((BLK, BLK), jnp.float32)
+    factor[bottom, top] = low
+    inverse[top, top] = upper_inverse
+    inverse[top, bottom] = jnp.zeros((BLK, BLK), jnp.float32)
+    a[...] = whole[bottom, bottom] - dot_full(low, low, ((1,), (1,)))
+    deal(1)
+    lower, lower_inverse = eliminate(a, w)
+    factor[bottom, bottom] = lower.T
+    inverse[bottom, bottom] = lower_inverse
+    inverse[bottom, top] = -dot_full(
+        lower_inverse, dot_full(factor[bottom, top], inverse[top, top], ((1,), (0,))),
+        ((1,), (0,)))
+    for part in range(2, PARTS):
+        deal(part)
+    for part in range(PARTS):
+        others(group, count, lambda k: row_wait(incoming.at[part, k], col_recv.at[part, k], k))
+    for part in range(PARTS):
+        others(prow, count, lambda k: row_copy(part, k).wait_send())
+        others(group, count, lambda k: col_copy(part, k).wait_send())
+    others(group, count, lambda k: scatter(k).wait_send())
+    others(prow, count, lambda k: across(k).wait_send())
+    others(group, count, lambda k: gather(k).wait_send())
+
+
+def exchange(rows, cols, lead_at, weight, outgoing, root_pivot):
+    count = COUNT
+    vmem = pl.BlockSpec(memory_space=pltpu.VMEM)
+    smem = pl.BlockSpec(memory_space=pltpu.SMEM)
+    shape = (PARTS, count, 2, SLOTS, PART, BLK)
+    piece = (RP // count, RP)
+    many = pltpu.SemaphoreType.DMA((count,))
+    pieces = pltpu.VMEM((count,) + piece, jnp.float32)
+    square = jax.ShapeDtypeStruct((RP, RP), jnp.float32)
     return pl.pallas_call(
-        deal_kernel,
-        out_shape=jax.ShapeDtypeStruct((groups, 2, slots, HALF, BLK), jnp.float32),
-        grid_spec=pltpu.PrefetchScalarGridSpec(
-            num_scalar_prefetch=2,
-            grid=(2, slots),
-            in_specs=[
-                pl.BlockSpec((1, HALF, width), lambda c, i, rows, cols: (rows[c, i], 0, 0))],
-            out_specs=pl.BlockSpec(
-                (groups, 1, 1, HALF, BLK), lambda c, i, rows, cols: (0, c, i, 0, 0)),
-        ),
-    )(rows, cols, arrived)
+        exchange_kernel,
+        out_shape=(jax.ShapeDtypeStruct(shape, jnp.float32), square, square),
+        in_specs=[smem, smem, smem, vmem, vmem, vmem],
+        out_specs=(vmem, vmem, vmem),
+        scratch_shapes=[pltpu.VMEM(shape, jnp.float32),
+                        pieces, pieces, pltpu.VMEM(piece, jnp.float32), pieces, pieces,
+                        pltpu.VMEM((BLK, BLK), jnp.float32), pltpu.VMEM((BLK, BLK), jnp.float32)]
+        + [pltpu.SemaphoreType.DMA((PARTS, count))] * 4 + [many] * 6
+        + [pltpu.VMEM(outgoing.shape[1:], jnp.float32)] * PARTS,
+        compiler_params=pltpu.CompilerParams(collective_id=3, has_side_effects=True),
+    )(rows, cols, lead_at, weight, outgoing, root_pivot.reshape((count,) + piece))
 
 
 def extend_kernel(source, row_there, col_there, root, *refs):
-    parts, (out, row_raw, col_raw) = refs[:4], refs[4:]
+    arrivals, (out, row_raw, col_raw) = refs[:4], refs[4:]
     column = pl.program_id(0)
     for slot in range(out.shape[0] // BLK):
         for half in range(2):
-            rows = pl.ds(slot * BLK + half * HALF, HALF)
-            value = root[rows, :]
-            for child in range(2):
-                there = row_there[child, slot] * col_there[child, column] > 0
-                part = parts[child * 2 + half][0, 0, slot]
-                value = value + jnp.where(there, part, 0.0)
-            out[rows, :] = value
-            if slot < RP // BLK:
-                col_raw[rows, :] = value
+            for part in range(PARTS):
+                rows = pl.ds(slot * BLK + half * HALF + part * PART, PART)
+                value = root[rows, :]
+                for child in range(2):
+                    there = row_there[child, slot] * col_there[child, column] > 0
+                    block = arrivals[child * 2 + half][part, 0, 0, slot]
+                    value = value + jnp.where(there, block, 0.0)
+                out[rows, :] = value
+                if slot < RP // BLK:
+                    col_raw[rows, :] = value
 
     @pl.when(column < RP // BLK)
     def _():
@@ -263,12 +505,12 @@
 def extend(source, row_there, col_there, root, incoming):
     rows, cols = root.shape
     slots = cols // BLK
-    groups = incoming.shape[0] // 2
+    groups = incoming.shape[1] // 2
 
     def part(child, half):
         return pl.BlockSpec(
-            (1, 1, rows // BLK, HALF, BLK),
-            lambda j, source, *_: (half * groups + source[child, j], child, 0, 0, 0))
+            (PARTS, 1, 1, rows // BLK, PART, BLK),
+            lambda j, source, *_: (0, half * groups + source[child, j], child, 0, 0, 0))
 
     column = pl.BlockSpec((rows, BLK), lambda j, *_: (0, j))
     return pl.pallas_call(
@@ -285,87 +527,6 @@
                        pl.BlockSpec((RP, BLK), lambda j, *_: (0, j))),
         ),
     )(source, row_there, col_there, root, *[incoming] * 4)
-
-
-def remote(source, target, send, recv, device):
-    return pltpu.make_async_remote_copy(
-        source, target, send, recv, device_id=device, device_id_type=MESH)
-
-
-def others(me, count, body):
-    @pl.loop(1, count)
-    def _(step):
-        body((me + step) % count)
-
-
-def neighbours():
-    half, prow, pcol = position()
-
-    def in_row(k):
-        return (k // 8, prow, k % 8)
-
-    def in_col(k):
-        return (half, k, pcol)
-
-    return half * 8 + pcol, prow, in_row, in_col
-
-
-def pivot_kernel(share, out, first, mid, second, first_send, first_recv, second_send,
-                 second_recv, third_send, third_recv):
-    count = 16
-    group, prow, in_row, in_col = neighbours()
-    greet([in_row((group + k) % count) for k in range(1, count)]
-          + [in_col((prow + k) % count) for k in range(1, count)])
-
-    def scatter(k):
-        return remote(share.at[k], first.at[group], first_send.at[k], first_recv.at[group],
-                      in_row(k))
-
-    def across(k):
-        return remote(mid, second.at[prow], second_send.at[k], second_recv.at[prow], in_col(k))
-
-    def gather(k):
-        return remote(out.at[group], out.at[group], third_send.at[k], third_recv.at[group],
-                      in_row(k))
-
-    def arrive(target, recv, k):
-        remote(target.at[k], target.at[k], recv.at[k], recv.at[k], in_row((group + 1) % count)).wait_recv()
-
-    others(group, count, lambda k: scatter(k).start())
-    first[group] = share[group]
-    others(group, count, lambda k: arrive(first, first_recv, k))
-    total = first[0]
-    for k in range(1, count):
-        total = total + first[k]
-    mid[...] = total
-    second[prow] = total
-    others(prow, count, lambda k: across(k).start())
-    others(prow, count, lambda k: arrive(second, second_recv, k))
-    total = second[0]
-    for k in range(1, count):
-        total = total + second[k]
-    out[group] = total
-    others(group, count, lambda k: gather(k).start())
-    others(group, count, lambda k: arrive(out, third_recv, k))
-    others(group, count, lambda k: scatter(k).wait_send())
-    others(prow, count, lambda k: across(k).wait_send())
-    others(group, count, lambda k: gather(k).wait_send())
-
-
-def pivot_sum(share):
-    count = 16
-    rows = RP // count
-    many = pltpu.SemaphoreType.DMA((count,))
-    vmem = pl.BlockSpec(memory_space=pltpu.VMEM)
-    pieces = pltpu.VMEM((count, rows, RP), jnp.float32)
-    return pl.pallas_call(
-        pivot_kernel,
-        out_shape=jax.ShapeDtypeStruct((count, rows, RP), jnp.float32),
-        in_specs=[vmem],
-        out_specs=vmem,
-        scratch_shapes=[pieces, pltpu.VMEM((rows, RP), jnp.float32), pieces] + [many] * 6,
-        compiler_params=pltpu.CompilerParams(collective_id=2, has_side_effects=True),
-    )(share.reshape(count, rows, RP)).reshape(RP, RP)
 
 
 def share_kernel(row_raw, col_raw, row_out, col_out, row_cast, row_in, row_send, row_recv,
@@ -470,61 +631,15 @@
     return row_out.reshape(rows, RP), col_out.reshape(RP, cols)
 
 
-def find(labels, wanted, values):
-    hit = labels[..., None, :] == wanted[:, None]
-    return jnp.sum(jnp.where(hit, values, 0), axis=-1).astype(jnp.int32), jnp.any(hit, axis=-1)
-
-
 def shards(child_update, child_panel, root_front, index_map):
-    rows_dev, cols_dev = child_update.shape[1:]
     root_rows, root_cols = root_front.shape
-    row_count, col_count, groups = 16, 8, 16
     row_index = lax.axis_index("prow")
-    col_index = lax.axis_index("pcol")
     group_index = lax.axis_index(("half", "pcol"))
-    row_slots, col_slots = root_rows // BLK, root_cols // BLK
-    child_blocks, col_blocks = rows_dev // BLK, cols_dev // BLK
-    blocks = jnp.arange(index_map.shape[1], dtype=jnp.int32)
-    everyone = jnp.arange(row_count, dtype=jnp.int32)
-
-    own_rows = lax.dynamic_slice_in_dim(index_map, row_index * child_blocks, child_blocks, 1)
-    leaves, _ = find(own_rows.reshape(-1) // row_slots, everyone,
-                     jnp.arange(2 * child_blocks, dtype=jnp.int32))
-    row_source, row_there = find(
-        index_map, row_index * row_slots + jnp.arange(row_slots, dtype=jnp.int32),
-        blocks // child_blocks)
-    own_cols = lax.dynamic_slice_in_dim(index_map, col_index * col_blocks, col_blocks, 1)
-    col_leaves, _ = find(own_cols // col_slots, everyone, jnp.arange(col_blocks, dtype=jnp.int32))
-    col_source, col_there = find(
-        index_map, group_index * col_slots + jnp.arange(col_slots, dtype=jnp.int32),
-        blocks // col_blocks)
-
+    leaves, rows, cols, lead_at, col_source, row_there, col_there, weight = tables(index_map)
     outgoing = spread(leaves, child_panel[0], child_update[0])
-    arrived = lax.all_to_all(outgoing, "prow", split_axis=0, concat_axis=0, tiled=True)
-
-    lead = own_rows.reshape(-1)
-    lead_hit = lead < RP // BLK
-    lead_row = jnp.sum(jnp.where(lead_hit, lead, 0))
-    lead_child = jnp.sum(jnp.where(lead_hit, jnp.arange(lead.shape[0]) // child_blocks, 0))
-    lead_cols = lax.dynamic_index_in_dim(own_cols, lead_child, 0, keepdims=False)
-    col_hit = lead_cols < RP // BLK
-    lead_col = jnp.sum(jnp.where(col_hit, lead_cols, 0))
-    lead_start = jnp.sum(jnp.where(col_hit, jnp.arange(col_blocks) * BLK, 0))
-    lead_block = lax.dynamic_slice(outgoing, (0, 0, lead_start), (1, HALF, BLK))[0]
-    lead_block = jnp.where(jnp.any(lead_hit) & jnp.any(col_hit), lead_block, 0.0)
-    lead_root = jnp.where((row_index == 0) & (group_index == 0), root_front[:RP, :RP], 0.0)
-    at = (lead_row * BLK + lax.axis_index("half") * HALF, lead_col * BLK)
-    lead_part = lax.dynamic_update_slice(
-        lead_root, lead_block + lax.dynamic_slice(lead_root, at, (HALF, BLK)), at)
-    pivot, arrived = lax.optimization_barrier((pivot_sum(lead_part), arrived))
-    factor = jnp.linalg.cholesky(pivot)
-    inverse = lax.linalg.triangular_solve(
-        factor, jnp.eye(RP, dtype=jnp.float32), left_side=True, lower=True)
-
-    dealt = deal(row_source, col_leaves, arrived, groups, row_slots)
-    incoming = lax.all_to_all(dealt, ("half", "pcol"), split_axis=0, concat_axis=0, tiled=True)
-    assembled, row_raw, col_raw = extend(
-        col_source, row_there.astype(jnp.int32), col_there.astype(jnp.int32), root_front, incoming)
+    incoming, factor, inverse = exchange(
+        rows, cols, lead_at, weight, outgoing, root_front[:RP, :RP])
+    assembled, row_raw, col_raw = extend(col_source, row_there, col_there, root_front, incoming)
     row_raw, col_raw = share(row_raw, col_raw)
 
     high = lax.Precision.HIGH

time: 357 us -> 301 us (0.84)
  other arithmetic: 65.2 us -> 3.01 us
  Pallas kernels: 224 us -> 283 us
  starting transfers between devices: 33.1 us -> 0 us
  waiting for transfers between devices: 11.1 us -> 0 us
  between operations: 7.85 us -> 0.1 us
    pallas_call x3, Pallas kernels: 174 us -> 235 us  [the longest x1 167 us: exchange(): pl.pallas_call(exchange_kernel, out_shape=(jax.ShapeDtypeStruct(shape, jn...]
    another operation x9 -> x0, other arithmetic: 53.9 us -> none  [the longest x6 34 us: shards(): factor = jnp.linalg.cholesky(pivot)]
    all_to_all x2 -> x0, starting transfers between devices: 33.1 us -> none  [the longest x1 28.2 us: shards(): lax.all_to_all(outgoing, 'prow', split_axis=0, concat_axis=0, tiled=True)]
    all_to_all x2 -> x0, waiting for transfers between devices: 11.1 us -> none  [the longest x1 11.1 us: shards(): lax.all_to_all(dealt, ('half', 'pcol'), split_axis=0, concat_axis=0, tile...]
    another operation x11 -> x0, local copies, waits for them, and re-layouts: 4.06 us -> none
    reduce_sum x5 -> x0, other arithmetic: 3.78 us -> none  [the longest x3 1.67 us: find(): jnp.sum(jnp.where(hit, values, 0), axis=-1).astype(jnp.int32)]
  transfers between devices with their start and end apart: 2 -> 0, of which waited for: 1 -> 0; matrix products, arithmetic and copies ran while one was open for 19% -> 0% of each run, Pallas kernels for 28% -> 0%
where the time goes in v3:
time: 301 us; the launch traced here: 297 us
  Pallas kernels  283 us (94%)
  matrix products  6.5 us (2%)
  local copies, waits for them, and re-layouts  4.44 us (1%)
    pallas_call x1, Pallas kernels, exchange(): pl.pallas_call(exchange_kernel, out_shape=(jax.ShapeDtypeStruct(shape, jn...  167 us
    pallas_call x1, Pallas kernels, spread(): pl.pallas_call(spread_kernel, out_shape=jax.ShapeDtypeStruct((PARTS, COUN...  64.8 us
    pallas_call x1, Pallas kernels, share(): pl.pallas_call(share_kernel, out_shape=(jax.ShapeDtypeStruct(row_shape, j...  40.9 us
    pallas_call x1, Pallas kernels, extend(): pl.pallas_call(extend_kernel, out_shape=(jax.ShapeDtypeStruct(root.shape,...  7.41 us

profile of v3, /device:TPU:4, one launch (start us, length us, event | category | flops | bytes accessed | tf_op | source)
XLA Modules:
  0.0 297.3 jit_solution(15495918521255550093)
XLA Ops:
  0.0 3.0 %shard_map.46 = (s32[1,16]{1,0:T(1,128)}, s32[2,6]{1,0:T(2,128)}, s32[2,16]{1,0:T(2,128)}, s32[1,1]{1,0:T(1,128)}, s32[2,6]{1,0:T(2,128)}, /*index=5*/s32[2,6]{1,0:T(2,128)}, s32[2,6]{1,0:T(2,128)}, f32[4,8,128]{2,1,0:T(8,128)}) custom-call(s32[2,64]{1,0:T(2,128)} %index_map.1), custom_call_target="tpu_custom_call" | custom-call | tf_op jit(solution)/shard_map/pallas_call | solution.py:125
  3.0 64.8 %shard_map.47.outgoing = f32[4,16,8,16,128]{4,3,2,1,0:T(8,128)} custom-call(s32[1,16]{1,0:T(1,128)} %get-tuple-element.25.leaves, f32[512,1024]{1,0:T(8,128)} %bitcast.13, f32[512,1024]{1,0:T(8,128)} %bitcast.14), custom_call_target="tpu_custom_call" | custom-call | tf_op jit(solution)/shard_map/pallas_call | solution.py:299
  67.8 1.7 slice.9
  69.4 167.1 %shard_map.48 = (f32[4,16,2,6,16,128]{5,4,3,2,1,0:T(8,128)}, f32[256,256]{1,0:T(8,128)}, f32[256,256]{1,0:T(8,128)}) custom-call(s32[2,6]{1,0:T(2,128)} %get-tuple-element.21.rows, s32[2,16]{1,0:T(2,128)} %get-tuple-element.22.cols, s32[1,1]{1,0:T(1,128)} %get-tuple-element.23.lead_at, f32[4,8,128]{2,1,0:T(8,128)} %get-tuple-element.24.weight, ...), custom_call_target="tpu_custom_call" | custom-call | tf_op jit(solution)/shard_map/pallas_call | solution.py:470
  236.6 0.0 copy-start.1
  236.6 7.4 %shard_map.49 = (f32[768,768]{1,0:T(8,128)}, f32[768,256]{1,0:T(8,128)}, f32[256,768]{1,0:T(8,128)}) custom-call(s32[2,6]{1,0:T(2,128)} %get-tuple-element.27.source, s32[2,6]{1,0:T(2,128)} %get-tuple-element.28.row_there, s32[2,6]{1,0:T(2,128)} %get-tuple-element.29.col_there, f32[768,768]{1,0:T(8,128)} %root.1, ...), custom_call_target="tpu_custom_call" | custom-call | tf_op jit(solution)/shard_map/pallas_call | solution.py:516
  244.0 40.9 %shard_map.50 = (f32[16,48,256]{2,1,0:T(8,128)}, f32[16,16,768]{2,1,0:T(8,128)}) custom-call(f32[16,48,256]{2,1,0:T(8,128)} %bitcast.18, f32[16,16,768]{2,1,0:T(8,128)} %bitcast.19), custom_call_target="tpu_custom_call" | custom-call | tf_op jit(solution)/shard_map/pallas_call | solution.py:622
  284.9 0.0 copy-start.2
  284.9 0.0 copy-done.1
  284.9 1.7 fusion.2
  286.7 0.0 copy-done.2
  286.7 1.4 fusion.3
  288.1 3.3 %select_subtract_fusion = f32[768,768]{1,0:T(8,128)S(1)} fusion(f32[768,768]{1,0:T(8,128)} %get-tuple-element.35, f32[768,256]{0,1:T(8,128)S(1)} %fusion.2, f32[256,768]{1,0:T(8,128)} %fusion.3, pred[768]{0:T(1024)(128)(4,1)S(1)} %add_compare_fusion, pred[768]{0:T(1024)(128)(4,1)S(1)} %get-tuple-element.37), kind=kOutput, calls=%fused_computation.1 | convolution fusion | flops 907739136 | bytes 6292992 | tf_op jit(solution)/shard_map/dot_general | solution.py:650
  291.5 0.0 copy-start.3
  291.5 1.4 slice.13
  292.9 1.2 copy.5
  294.0 0.0 copy-done.3
  294.0 0.0 copy-start
  294.0 1.4 slice_select_fusion
  295.5 0.2 copy-done
  295.7 1.6 pad_maximum_fusion
  (2 shorter events, 0.0 us)
Async XLA Ops:
  236.6 48.4 %copy-start.1 = (f32[256,256]{1,0:T(8,128)S(1)}, f32[256,256]{1,0:T(8,128)}, u32[]{:S(2)}) copy-start(f32[256,256]{1,0:T(8,128)} %get-tuple-element.34) | copy-start | bytes 786436
  284.9 1.7 copy-start.2
  291.5 2.5 copy-start.3
  294.0 1.6 copy-start

commit v4 on v3

--- a/solution.py
+++ b/solution.py
@@ -72,7 +72,8 @@
             table[i, j] = value
 
 
-def tables_kernel(index_map, leaves, rows, cols, lead_at, source, row_there, col_there, weight):
+def tables_kernel(index_map, leaves, rows, cols, lead_at, source, weight, there,
+                  row_there, col_there):
     group, prow, _, _ = neighbours()
     pcol = lax.axis_index("pcol")
     total = index_map.shape[1]
@@ -116,18 +117,26 @@
         for j in range(RP // BLK):
             hit = jnp.where((lead == i) & (cross == j), 1.0, 0.0)
             weight[i * (RP // BLK) + j] = jnp.full(weight.shape[1:], hit, jnp.float32)
+    for child in range(2):
+        for i in range(SLOTS):
+            for j in range(SLOTS):
+                hit = jnp.where(row_there[child, i] * col_there[child, j] > 0, 1.0, 0.0)
+                there[(child * SLOTS + i) * SLOTS + j] = jnp.full(
+                    there.shape[1:], hit, jnp.float32)
 
 
 def tables(index_map):
     smem = pl.BlockSpec(memory_space=pltpu.SMEM)
     vmem = pl.BlockSpec(memory_space=pltpu.VMEM)
-    shapes = [(1, COUNT), (2, SLOTS), (2, COUNT), (1, 1)] + [(2, SLOTS)] * 3
+    shapes = [(1, COUNT), (2, SLOTS), (2, COUNT), (1, 1), (2, SLOTS)]
+    factors = [((RP // BLK) ** 2, 8, BLK), (2 * SLOTS * SLOTS, 8, BLK)]
     return pl.pallas_call(
         tables_kernel,
         out_shape=[jax.ShapeDtypeStruct(shape, jnp.int32) for shape in shapes]
-        + [jax.ShapeDtypeStruct(((RP // BLK) ** 2, 8, BLK), jnp.float32)],
+        + [jax.ShapeDtypeStruct(shape, jnp.float32) for shape in factors],
         in_specs=[smem],
-        out_specs=[smem] * len(shapes) + [vmem],
+        out_specs=[smem] * len(shapes) + [vmem] * len(factors),
+        scratch_shapes=[pltpu.SMEM((2, SLOTS), jnp.int32)] * 2,
     )(index_map)
 
 
@@ -345,10 +354,11 @@
                            preferred_element_type=jnp.float32)
 
 
-def exchange_kernel(rows, cols, lead_at, weight, outgoing, root_pivot, incoming, factor,
-                    inverse, dealt, share, first, mid, second, pivot, a, w, row_send, row_recv,
-                    col_send, col_recv, first_send, first_recv, second_send, second_recv,
-                    third_send, third_recv, *arrived):
+def exchange_kernel(rows, cols, lead_at, source, weight, there, outgoing, root, out, incoming,
+                    factor, inverse, dealt, share, first, mid, second, pivot, a, w, row_panel,
+                    col_panel, row_send, row_recv, col_send, col_recv, first_send, first_recv,
+                    second_send, second_recv, third_send, third_recv, over_cast, over_in,
+                    over_send, over_recv, down_cast, down_in, down_send, down_recv, *arrived):
     count = COUNT
     core = lax.axis_index("half")
     group, prow, in_row, in_col = neighbours()
@@ -399,7 +409,8 @@
           + [in_col((prow + k) % count) for k in range(1, count)])
     send_rows(0)
 
-    share[...] = jnp.where((group == 0) & (prow == 0), root_pivot[...], 0.0)
+    share[...] = jnp.where(
+        (group == 0) & (prow == 0), root[:RP, :RP].reshape(share.shape), 0.0)
     for part in range(PARTS):
         block = outgoing[part, 0, lead_at[0, 0]]
         for i in range(RP // BLK):
@@ -450,6 +461,116 @@
         deal(part)
     for part in range(PARTS):
         others(group, count, lambda k: row_wait(incoming.at[part, k], col_recv.at[part, k], k))
+
+    def add(i, j):
+        here = pl.ds(pl.multiple_of(j * BLK, BLK), BLK)
+        for half in range(2):
+            for part in range(PARTS):
+                start = pl.multiple_of(i * BLK + half * HALF + part * PART, PART)
+                value = root[pl.ds(start, PART), here]
+                for child in range(2):
+                    scale = there[(child * SLOTS + i) * SLOTS + j, 0:1, :]
+                    value = value + incoming[part, half * 8 + source[child, j], child, i] * scale
+                out[pl.ds(start, PART), here] = value
+
+    edge = RP // BLK
+    size = SLOTS * BLK
+
+    @pl.loop(0, SLOTS * edge)
+    def _(item):
+        add(item // edge, item % edge)
+
+    @pl.loop(0, (SLOTS - edge) * edge)
+    def _(item):
+        add(item % edge, edge + item // edge)
+
+    over, under = size // count, RP // count
+
+    def cut(ref, k, lines):
+        return ref.at[pl.ds(pl.multiple_of(k * lines, lines), lines)]
+
+    def over_first(k):
+        return remote(cut(row_panel, k, over), cut(row_panel, k, over), over_cast.at[k], over_in,
+                      in_row(k))
+
+    def over_second(k):
+        return remote(cut(row_panel, group, over), cut(row_panel, group, over), over_send.at[k],
+                      over_recv.at[group], in_row(k))
+
+    def down_first(k):
+        return remote(cut(col_panel, k, under), cut(col_panel, k, under), down_cast.at[k],
+                      down_in, in_col(k))
+
+    def down_second(k):
+        return remote(cut(col_panel, prow, under), cut(col_panel, prow, under), down_send.at[k],
+                      down_recv.at[prow], in_col(k))
+
+    def spare_first(k, body):
+        @pl.when(k > 0)
+        def _():
+            body()
+
+    @pl.when(prow == 0)
+    def _():
+        col_panel[...] = out[:RP, :]
+        others(prow, count, lambda k: down_first(k).start())
+        others(prow, count, lambda k: down_second(k).start())
+
+    @pl.when(group == 0)
+    def _():
+        row_panel[...] = out[:, :RP]
+        others(group, count, lambda k: over_first(k).start())
+        others(group, count, lambda k: over_second(k).start())
+
+    @pl.loop(0, (SLOTS - edge) * (SLOTS - edge))
+    def _(item):
+        add(edge + item // (SLOTS - edge), edge + item % (SLOTS - edge))
+
+    @pl.when(group > 0)
+    def _():
+        over_first(group).wait_recv()
+        others(group, count, lambda k: spare_first(k, lambda: over_second(k).start()))
+
+    @pl.when(prow > 0)
+    def _():
+        down_first(prow).wait_recv()
+        others(prow, count, lambda k: spare_first(k, lambda: down_second(k).start()))
+
+    @pl.when(group > 0)
+    def _():
+        others(group, count, lambda k: row_wait(cut(row_panel, k, over), over_recv.at[k], k))
+
+    solver = split(inverse[...])
+    left = dot3(split(row_panel[...]), solver, ((1,), (1,)))
+
+    @pl.when(prow > 0)
+    def _():
+        others(prow, count, lambda k: col_wait(cut(col_panel, k, under), down_recv.at[k], k))
+
+    left_parts = split(left)
+    for tile in range(size // RP):
+        here = slice(tile * RP, (tile + 1) * RP)
+        right = dot3(solver, split(col_panel[:, here]), ((1,), (0,)))
+        trailing = out[:, here] - dot3(left_parts, split(right), ((1,), (0,)))
+        upper_rows = jnp.where(prow > 0, trailing[:RP], out[:RP, here])
+        lower_rows = trailing[RP:]
+        if tile == 0:
+            panel_rows = jnp.where(prow > 0, left[:RP], factor[...])
+            upper_rows = jnp.where(group > 0, upper_rows, panel_rows)
+            lower_rows = jnp.where(group > 0, lower_rows, left[RP:])
+        out[:RP, here] = upper_rows
+        out[RP:, here] = lower_rows
+
+    @pl.when(group == 0)
+    def _():
+        others(group, count, lambda k: over_first(k).wait_send())
+
+    @pl.when(prow == 0)
+    def _():
+        others(prow, count, lambda k: down_first(k).wait_send())
+
+    others(group, count, lambda k: spare_first(k, lambda: over_second(k).wait_send()))
+    others(prow, count, lambda k: spare_first(k, lambda: down_second(k).wait_send()))
     for part in range(PARTS):
         others(prow, count, lambda k: row_copy(part, k).wait_send())
         others(group, count, lambda k: col_copy(part, k).wait_send())
@@ -458,202 +579,37 @@
     others(group, count, lambda k: gather(k).wait_send())
 
 
-def exchange(rows, cols, lead_at, weight, outgoing, root_pivot):
+def exchange(rows, cols, lead_at, source, weight, there, outgoing, root):
     count = COUNT
     vmem = pl.BlockSpec(memory_space=pltpu.VMEM)
     smem = pl.BlockSpec(memory_space=pltpu.SMEM)
     shape = (PARTS, count, 2, SLOTS, PART, BLK)
     piece = (RP // count, RP)
-    many = pltpu.SemaphoreType.DMA((count,))
+    one, many = pltpu.SemaphoreType.DMA, pltpu.SemaphoreType.DMA((count,))
     pieces = pltpu.VMEM((count,) + piece, jnp.float32)
-    square = jax.ShapeDtypeStruct((RP, RP), jnp.float32)
+    square = pltpu.VMEM((RP, RP), jnp.float32)
+    corner = pltpu.VMEM((BLK, BLK), jnp.float32)
     return pl.pallas_call(
         exchange_kernel,
-        out_shape=(jax.ShapeDtypeStruct(shape, jnp.float32), square, square),
-        in_specs=[smem, smem, smem, vmem, vmem, vmem],
-        out_specs=(vmem, vmem, vmem),
-        scratch_shapes=[pltpu.VMEM(shape, jnp.float32),
+        out_shape=jax.ShapeDtypeStruct(root.shape, jnp.float32),
+        in_specs=[smem, smem, smem, smem, vmem, vmem, vmem, vmem],
+        out_specs=vmem,
+        scratch_shapes=[pltpu.VMEM(shape, jnp.float32), square, square,
+                        pltpu.VMEM(shape, jnp.float32),
                         pieces, pieces, pltpu.VMEM(piece, jnp.float32), pieces, pieces,
-                        pltpu.VMEM((BLK, BLK), jnp.float32), pltpu.VMEM((BLK, BLK), jnp.float32)]
+                        corner, corner, pltpu.VMEM((root.shape[0], RP), jnp.float32),
+                        pltpu.VMEM((RP, root.shape[1]), jnp.float32)]
         + [pltpu.SemaphoreType.DMA((PARTS, count))] * 4 + [many] * 6
+        + [many, one, many, many] * 2
         + [pltpu.VMEM(outgoing.shape[1:], jnp.float32)] * PARTS,
         compiler_params=pltpu.CompilerParams(collective_id=3, has_side_effects=True),
-    )(rows, cols, lead_at, weight, outgoing, root_pivot.reshape((count,) + piece))
-
-
-def extend_kernel(source, row_there, col_there, root, *refs):
-    arrivals, (out, row_raw, col_raw) = refs[:4], refs[4:]
-    column = pl.program_id(0)
-    for slot in range(out.shape[0] // BLK):
-        for half in range(2):
-            for part in range(PARTS):
-                rows = pl.ds(slot * BLK + half * HALF + part * PART, PART)
-                value = root[rows, :]
-                for child in range(2):
-                    there = row_there[child, slot] * col_there[child, column] > 0
-                    block = arrivals[child * 2 + half][part, 0, 0, slot]
-                    value = value + jnp.where(there, block, 0.0)
-                out[rows, :] = value
-                if slot < RP // BLK:
-                    col_raw[rows, :] = value
-
-    @pl.when(column < RP // BLK)
-    def _():
-        row_raw[...] = out[...]
-
-
-def extend(source, row_there, col_there, root, incoming):
-    rows, cols = root.shape
-    slots = cols // BLK
-    groups = incoming.shape[1] // 2
-
-    def part(child, half):
-        return pl.BlockSpec(
-            (PARTS, 1, 1, rows // BLK, PART, BLK),
-            lambda j, source, *_: (0, half * groups + source[child, j], child, 0, 0, 0))
-
-    column = pl.BlockSpec((rows, BLK), lambda j, *_: (0, j))
-    return pl.pallas_call(
-        extend_kernel,
-        out_shape=(jax.ShapeDtypeStruct(root.shape, jnp.float32),
-                   jax.ShapeDtypeStruct((rows, RP), jnp.float32),
-                   jax.ShapeDtypeStruct((RP, cols), jnp.float32)),
-        grid_spec=pltpu.PrefetchScalarGridSpec(
-            num_scalar_prefetch=3,
-            grid=(slots,),
-            in_specs=[column] + [part(c, h) for c in range(2) for h in range(2)],
-            out_specs=(column,
-                       pl.BlockSpec((rows, BLK), lambda j, *_: (0, jnp.minimum(j, RP // BLK - 1))),
-                       pl.BlockSpec((RP, BLK), lambda j, *_: (0, j))),
-        ),
-    )(source, row_there, col_there, root, *[incoming] * 4)
-
-
-def share_kernel(row_raw, col_raw, row_out, col_out, row_cast, row_in, row_send, row_recv,
-                 col_cast, col_in, col_send, col_recv):
-    count = 16
-    group, prow, in_row, in_col = neighbours()
-    greet([in_row((group + k) % count) for k in range(1, count)]
-          + [in_col((prow + k) % count) for k in range(1, count)])
-
-    def row_first(k):
-        return remote(row_raw.at[k], row_out.at[k], row_cast.at[k], row_in, in_row(k))
-
-    def row_second(k):
-        return remote(row_out.at[group], row_out.at[group], row_send.at[k], row_recv.at[group],
-                      in_row(k))
-
-    def col_first(k):
-        return remote(col_raw.at[k], col_out.at[k], col_cast.at[k], col_in, in_col(k))
-
-    def col_second(k):
-        return remote(col_out.at[prow], col_out.at[prow], col_send.at[k], col_recv.at[prow],
-                      in_col(k))
-
-    def row_start(k):
-        return remote(row_raw.at[0], row_out.at[0], row_send.at[k], row_recv.at[0], in_row(k))
-
-    def col_start(k):
-        return remote(col_raw.at[0], col_out.at[0], col_send.at[k], col_recv.at[0], in_col(k))
-
-    def spare_first(k, body):
-        @pl.when(k > 0)
-        def _():
-            body()
-
-    @pl.when(group == 0)
-    def _():
-        others(group, count, lambda k: row_first(k).start())
-
-    @pl.when(prow == 0)
-    def _():
-        others(prow, count, lambda k: col_first(k).start())
-
-    @pl.when(group == 0)
-    def _():
-        others(group, count, lambda k: row_start(k).start())
-        row_out[...] = row_raw[...]
-
-    @pl.when(prow == 0)
-    def _():
-        others(prow, count, lambda k: col_start(k).start())
-        col_out[...] = col_raw[...]
-
-    @pl.when(group > 0)
-    def _():
-        row_first(group).wait_recv()
-        others(group, count, lambda k: spare_first(k, lambda: row_second(k).start()))
-
-    @pl.when(prow > 0)
-    def _():
-        col_first(prow).wait_recv()
-        others(prow, count, lambda k: spare_first(k, lambda: col_second(k).start()))
-
-    def arrive(target, recv, k):
-        remote(target.at[k], target.at[k], recv.at[k], recv.at[k], in_row((group + 1) % count)).wait_recv()
-
-    @pl.when(group > 0)
-    def _():
-        others(group, count, lambda k: arrive(row_out, row_recv, k))
-
-    @pl.when(prow > 0)
-    def _():
-        others(prow, count, lambda k: arrive(col_out, col_recv, k))
-
-    @pl.when(group == 0)
-    def _():
-        others(group, count, lambda k: row_first(k).wait_send())
-
-    @pl.when(prow == 0)
-    def _():
-        others(prow, count, lambda k: col_first(k).wait_send())
-
-    others(group, count, lambda k: spare_first(k, lambda: row_second(k).wait_send()))
-    others(prow, count, lambda k: spare_first(k, lambda: col_second(k).wait_send()))
-
-
-def share(row_raw, col_raw):
-    count = 16
-    one, many = pltpu.SemaphoreType.DMA, pltpu.SemaphoreType.DMA((count,))
-    vmem = pl.BlockSpec(memory_space=pltpu.VMEM)
-    rows, cols = row_raw.shape[0], col_raw.shape[1]
-    row_shape = (count, rows // count, RP)
-    col_shape = (count, RP // count, cols)
-    row_out, col_out = pl.pallas_call(
-        share_kernel,
-        out_shape=(jax.ShapeDtypeStruct(row_shape, jnp.float32),
-                   jax.ShapeDtypeStruct(col_shape, jnp.float32)),
-        in_specs=[vmem, vmem],
-        out_specs=(vmem, vmem),
-        scratch_shapes=[many, one, many, many, many, one, many, many],
-        compiler_params=pltpu.CompilerParams(collective_id=1, has_side_effects=True),
-    )(row_raw.reshape(row_shape), col_raw.reshape(col_shape))
-    return row_out.reshape(rows, RP), col_out.reshape(RP, cols)
+    )(rows, cols, lead_at, source, weight, there, outgoing, root)
 
 
 def shards(child_update, child_panel, root_front, index_map):
-    root_rows, root_cols = root_front.shape
-    row_index = lax.axis_index("prow")
-    group_index = lax.axis_index(("half", "pcol"))
-    leaves, rows, cols, lead_at, col_source, row_there, col_there, weight = tables(index_map)
+    leaves, rows, cols, lead_at, source, weight, there = tables(index_map)
     outgoing = spread(leaves, child_panel[0], child_update[0])
-    incoming, factor, inverse = exchange(
-        rows, cols, lead_at, weight, outgoing, root_front[:RP, :RP])
-    assembled, row_raw, col_raw = extend(col_source, row_there, col_there, root_front, incoming)
-    row_raw, col_raw = share(row_raw, col_raw)
-
-    high = lax.Precision.HIGH
-    global_rows = row_index * root_rows + jnp.arange(root_rows, dtype=jnp.int32)
-    global_cols = group_index * root_cols + jnp.arange(root_cols, dtype=jnp.int32)
-    left = lax.dot_general(row_raw, inverse, (((1,), (1,)), ((), ())), precision=high)
-    right = lax.dot_general(inverse, col_raw, (((1,), (0,)), ((), ())), precision=high)
-    update = lax.dot_general(left, right, (((1,), (0,)), ((), ())), precision=high)
-    trailing_mask = (global_rows[:, None] >= RP) & (global_cols[None, :] >= RP)
-    trailing = assembled - jnp.where(trailing_mask, update, 0.0)
-    leading = jnp.pad(factor, ((0, root_rows - RP), (0, 0)))
-    panel = jnp.where(global_rows[:, None] < RP, leading, left)
-    panel_cols = jnp.where(group_index == 0, panel, trailing[:, :RP])
-    return jnp.concatenate([panel_cols, trailing[:, RP:]], axis=1)
+    return exchange(rows, cols, lead_at, source, weight, there, outgoing, root_front)
 
 
 def solution(mesh):

time: 301 us -> 277 us (0.920)
  Pallas kernels: 283 us -> 269 us
  matrix products: 6.5 us -> 0 us
    pallas_call x3 -> x1, Pallas kernels: 215 us -> 201 us  [exchange(): pl.pallas_call(exchange_kernel, out_shape=jax.ShapeDtypeStruct(root.shape...]
    dot_general x3 -> x0, matrix products: 6.5 us -> none  [the longest x1 3.35 us: shards(): lax.dot_general(left, right, (((1,), (0,)), ((), ())), precision=high)]
    slice x2 -> x0, local copies, waits for them, and re-layouts: 3.05 us -> none  [the longest x1 1.67 us: shards(): root_front[:RP, :RP]]
where the time goes in v4:
time: 277 us; the launch traced here: 272 us
  Pallas kernels  269 us (97%)
  local copies, waits for them, and re-layouts  3.22 us (1%)
    pallas_call x1, Pallas kernels, exchange(): pl.pallas_call(exchange_kernel, out_shape=jax.ShapeDtypeStruct(root.shape...  201 us
    pallas_call x1, Pallas kernels, spread(): pl.pallas_call(spread_kernel, out_shape=jax.ShapeDtypeStruct((PARTS, COUN...  64.7 us

profile of v4, /device:TPU:4, one launch (start us, length us, event | category | flops | bytes accessed | tf_op | source)
XLA Modules:
  0.0 272.4 jit_solution(9558310185702522739)
XLA Ops:
  0.0 3.2 %shard_map.46 = (s32[1,16]{1,0:T(1,128)}, s32[2,6]{1,0:T(2,128)}, s32[2,16]{1,0:T(2,128)}, s32[1,1]{1,0:T(1,128)}, s32[2,6]{1,0:T(2,128)}, /*index=5*/f32[4,8,128]{2,1,0:T(8,128)}, f32[72,8,128]{2,1,0:T(8,128)}) custom-call(s32[2,64]{1,0:T(2,128)} %index_map.1), custom_call_target="tpu_custom_call" | custom-call | tf_op jit(solution)/shard_map/pallas_call | solution.py:133
  3.2 64.7 %shard_map.47.outgoing = f32[4,16,8,16,128]{4,3,2,1,0:T(8,128)} custom-call(s32[1,16]{1,0:T(1,128)} %get-tuple-element.18.leaves, f32[512,1024]{1,0:T(8,128)} %bitcast.2, f32[512,1024]{1,0:T(8,128)} %bitcast.3), custom_call_target="tpu_custom_call" | custom-call | tf_op jit(solution)/shard_map/pallas_call | solution.py:308
  67.9 201.3 %shard_map.48 = f32[768,768]{1,0:T(8,128)} custom-call(s32[2,6]{1,0:T(2,128)} %get-tuple-element.12.rows, s32[2,16]{1,0:T(2,128)} %get-tuple-element.13.cols, s32[1,1]{1,0:T(1,128)} %get-tuple-element.14.lead_at, s32[2,6]{1,0:T(2,128)} %get-tuple-element.15.source, f32[4,8,128]{2,1,0:T(8,128)} %get-tuple-element.16.weight, ...), custom_call_target="tpu_custom_call" | custom-call | tf_op jit(solution)/shard_map/pallas_call | solution.py:592
  269.2 3.2 %copy.6 = f32[768,768]{1,0:T(8,128)} copy(f32[768,768]{1,0:T(8,128)} %shard_map.48) | data formatting | bytes 4718592
